TPU v7x, 32 devices: a whole 2x2x4 slice. The times are simulated.
32 devices in a mesh: groups: 2 (over x), gx: 16 (over z, y, core).
Axes of the slice: x: 2, y: 2, z: 4, core: 2. Of those that a mesh axis runs over, the one named last changes fastest.
Arguments:
- features: bfloat16 [128, 8, 8, 8, 128], P(('groups', 'gx')), parts along dimension 0, may hold values from -6 to 6
- fine_nbr: int32 [128, 27], P(('groups', 'gx')), parts along dimension 0, may hold values from -1 to 3, as said below
- fine_send: int32 [32, 2, 4], P(('groups', 'gx')), parts along dimension 0, may hold values from -1 to 3, as said below
- fine_parent: int32 [128], P(('groups', 'gx')), parts along dimension 0, may hold values from -1 to 127, as said below
- coarse_child: int32 [32, 8], P(('groups', 'gx')), parts along dimension 0, may hold values from -1 to 63, as said below
- coarse_nbr: int32 [32, 27], P(('groups', 'gx')), parts along dimension 0, may hold values from -1 to 15, as said below
- enc_fine_w: bfloat16 [27, 128, 128], replicated, may hold values from -0.15625 to 0.15625
- enc_coarse_w: bfloat16 [27, 128, 128], replicated, may hold values from -0.15625 to 0.15625
- dec_coarse_w: bfloat16 [27, 128, 128], replicated, may hold values from -0.15625 to 0.15625
- dec_fine_w: bfloat16 [27, 128, 128], replicated, may hold values from -0.15625 to 0.15625
Outputs:
- fine_out: bfloat16 [128, 8, 8, 8, 128], P(('groups', 'gx')), parts along dimension 0
There are 2 independent parts, one for each index of `groups`. A program takes and returns all parts, laid end to end along the dimension named above; an argument that names none is the same for every part. Nothing has to cross between parts.
Inputs may be any that keep to these rules, and one draw needn't show every extreme that they name: `fine_nbr`: entry t of a fine slot on gx device d names the slot, on device d + dx, of the brick at brick offset (dx, dy, dz), or is -1 where there is none. A slot whose entry 13 is -1 holds no brick and all its entries are -1; entry 13 of a brick is its own slot. Adjacency is symmetric. `fine_send`: on device d, entry s of row 0 is s when slot s holds a brick with a neighbour on device d + 1, else -1; row 1 likewise for device d - 1. `fine_parent`: 8 g + o for a brick whose parent is coarse slot g at octant o, -1 for slots without a brick. Coarse slot g is held by gx device g, which lies in the same aligned group of four gx devices as the child's device. `coarse_child`: entry o of coarse slot g is the fine slot f with fine_parent[f] = 8 g + o, or -1 where there is none. `coarse_nbr`: entry t (taps ordered as for fine_nbr) is the coarse slot of the neighbouring coarse brick, or -1 where there is none; entry 13 is the brick's own slot; every neighbour is held by a gx device of the same or an adjacent aligned group of four, and neighbours with dx = 0 by a device of the same aligned group of four.
All inputs are finite; a program needn't handle non-finite values.
Results may differ from a plain program's by a relative error of at most 0.01.
Values may be sent and summed in bfloat16 or wider, within the bound.
A program may use at most 128 MiB of HBM per device.

v0:
```python
import functools

import jax
import jax.numpy as jnp
from jax import lax
from jax.experimental import pallas as pl
from jax.experimental.pallas import tpu as pltpu
from jax.sharding import PartitionSpec as P

F32 = jnp.float32
BF16 = jnp.bfloat16
LANES = 4
MESH = pl.DeviceIdType.MESH


def pick(offset, edge):
    if offset < 0:
        return slice(edge - 1, edge)
    if offset == 0:
        return slice(0, edge)
    return slice(0, 1)


def place(offset, edge, base):
    if offset < 0:
        return slice(base - 1, base)
    if offset == 0:
        return slice(base, base + edge)
    return slice(base + edge, base + edge + 1)


def kernel(
    n,
    fine_nbr,
    fine_send,
    fine_parent,
    child_ref,
    nbr_ref,
    feat_hbm,
    w1_hbm,
    w2_hbm,
    w3_hbm,
    w4_hbm,
    out_ref,
    feat,
    w1,
    w2,
    w3,
    w4,
    pad,
    cols,
    opened,
    table,
    enc,
    below,
    above,
    face_out,
    face_in,
    face_out2,
    face_in2,
    half_z,
    pooled,
    pooled_out,
    children,
    meta,
    meta_s,
    coarse,
    coarse2,
    low_x,
    high_x,
    side_out,
    side_in,
    side_out2,
    side_in2,
    spread,
    lifted,
    load_sem,
    face_send_sem,
    face_recv_sem,
    pool_send_sem,
    pool_recv_sem,
    meta_send_sem,
    meta_recv_sem,
    side_send_sem,
    side_recv_sem,
    meta_sem,
):
    slots, edge = out_ref.shape[0], enc.shape[1]
    plane = edge * edge
    width = out_ref.shape[-1]
    half = edge // 2
    block = half**3
    per = child_ref.shape[0]
    bricks = LANES * per
    me = lax.axis_index("gx")
    member = lax.rem(me, LANES)
    group = lax.div(me, LANES)

    def peer(k):
        return me - member + (member ^ k)

    width = out_ref.shape[-1]
    loads = [[pltpu.make_async_copy(feat_hbm, feat, load_sem.at[0, 0])]]
    for i, (src, dst) in enumerate(
        ((w1_hbm, w1), (w2_hbm, w2), (w3_hbm, w3), (w4_hbm, w4))
    ):
        loads.append(
            [
                pltpu.make_async_copy(
                    src.at[dx], dst.at[:, dx * width : (dx + 1) * width], load_sem.at[i + 1, dx]
                )
                for dx in range(3)
            ]
        )
    for copies in loads:
        for copy in copies:
            copy.start()

    def loaded(i):
        for copy in loads[i]:
            copy.wait()

    has_prev, has_next = me > 0, me < n - 1
    has_down, has_up = me >= LANES, me < n - LANES
    barrier = pltpu.get_barrier_semaphore()

    def greet(other):
        pl.semaphore_signal(barrier, inc=1, device_id={"gx": other}, device_id_type=MESH)

    sides = (
        (has_prev & (member == 0), me - 1),
        (has_next & (member == LANES - 1), me + 1),
        (has_down, me - LANES),
        (has_up, me + LANES),
    )
    for k in range(1, LANES):
        greet(peer(k))
    peers = LANES - 1
    for there, other in sides:
        pl.when(there)(functools.partial(greet, other))
        peers = peers + jnp.where(there, 1, 0)
    pl.semaphore_wait(barrier, peers)

    def remote(src, dst, send, recv, other):
        return pltpu.make_async_remote_copy(
            src_ref=src,
            dst_ref=dst,
            send_sem=send,
            recv_sem=recv,
            device_id={"gx": other},
            device_id_type=MESH,
        )

    def face_copies(outgoing, incoming, phase):
        up = remote(
            outgoing.at[0],
            incoming.at[0],
            face_send_sem.at[phase, 0],
            face_recv_sem.at[phase, 0],
            me + 1,
        )
        down = remote(
            outgoing.at[1],
            incoming.at[1],
            face_send_sem.at[phase, 1],
            face_recv_sem.at[phase, 1],
            me - 1,
        )
        return up, down

    def start_pair(up, up_there, down, down_there):
        pl.when(up_there)(up.start)
        pl.when(down_there)(down.start)

    def finish_pair(up, up_there, down, down_there):
        @pl.when(down_there)
        def _():
            up.wait_recv()
            down.wait_send()

        @pl.when(up_there)
        def _():
            down.wait_recv()
            up.wait_send()

    meta[member, 0:per, 0 : child_ref.shape[1]] = child_ref[...]
    meta[member, per : 2 * per, 0 : nbr_ref.shape[1]] = nbr_ref[...]

    cube = (edge, edge, edge, width)
    zero_brick = jnp.zeros(cube, F32)
    zero_plane = jnp.zeros((edge, edge, width), F32)
    table[slots] = zero_brick

    def stage_faces(outgoing, s):
        up_from = jnp.where(fine_send[0, s] >= 0, s, slots)
        down_from = jnp.where(fine_send[1, s] >= 0, s, slots)
        outgoing[0, s] = table[up_from, edge - 1].reshape(plane, width).astype(BF16)
        outgoing[1, s] = table[down_from, 0].reshape(plane, width).astype(BF16)

    loaded(0)
    for s in range(slots):
        table[s] = feat[s].astype(F32).reshape(cube)
    for s in range(slots):
        stage_faces(face_out, s)
    halo1 = face_copies(face_out, face_in, 0)
    start_pair(halo1[0], has_next, halo1[1], has_prev)
    meta_copies = [
        remote(
            meta.at[member],
            meta.at[member],
            meta_send_sem.at[k - 1],
            meta_recv_sem.at[k - 1],
            peer(k),
        )
        for k in range(1, LANES)
    ]
    for copy in meta_copies:
        copy.start()

    below[slots] = zero_plane
    above[slots] = zero_plane
    coarse[bricks] = zero_brick
    coarse2[bricks] = zero_brick
    low_x[3 * bricks] = zero_plane
    high_x[3 * bricks] = zero_plane
    children[LANES * slots] = jnp.zeros((block, width), F32)

    base = edge

    def assemble(centre, lower, upper, index, taps=range(27)):
        for t in taps:
            dx, dy, dz = t // 9 - 1, t // 3 % 3 - 1, t % 3 - 1
            at = index(t)
            ys, zs = pick(dy, edge), pick(dz, edge)
            if dx == 0:
                piece = centre[at, :, ys, zs, :]
            elif dx < 0:
                piece = lower[at, ys, zs, :][None]
            else:
                piece = upper[at, ys, zs, :][None]
            pad[place(dx, edge, 1), place(dy, edge, 1), place(dz, edge, base), :] = piece

    def product(weights, planes, rows):
        two = jnp.dot(
            cols[0 : (planes + 1) * rows, :],
            weights[:, 0 : 2 * width],
            preferred_element_type=F32,
        )
        third = jnp.dot(
            cols[2 * rows : (planes + 2) * rows, :],
            weights[:, 2 * width : 3 * width],
            preferred_element_type=F32,
        )
        total = third + two[0 : planes * rows, 0:width] + two[rows:, width : 2 * width]
        return jnp.maximum(total, 0.0).astype(BF16)

    own_taps = range(9, 18)
    far_taps = (*range(9), *range(18, 27))

    def gather_columns(x, row):
        for k in range(9):
            dy, dz = k // 3, k % 3 - 1
            piece = pad[x, dy : dy + edge, base + dz : base + dz + edge, :]
            cols[pl.ds(row, plane), k * width : (k + 1) * width] = piece.reshape(
                plane, width
            ).astype(BF16)

    def local_product(centre, j, index, weights):
        assemble(centre, None, None, index, own_taps)
        for x in range(edge):
            gather_columns(x + 1, x * plane)
        two = jnp.dot(
            cols[0 : edge * plane, :], weights[:, 0 : 2 * width], preferred_element_type=F32
        )
        third = jnp.dot(
            cols[plane : edge * plane, :],
            weights[:, 2 * width : 3 * width],
            preferred_element_type=F32,
        )
        inner = slice(plane, (edge - 1) * plane)
        middle = two[:, width : 2 * width]
        opened[j, 0] = middle[0:plane] + third[0:plane]
        opened[j, 1] = middle[(edge - 1) * plane :] + two[(edge - 2) * plane : (edge - 1) * plane, 0:width]
        total = middle[inner] + third[inner] + two[0 : (edge - 2) * plane, 0:width]
        return jnp.maximum(total, 0.0).astype(BF16)

    def outer_planes(count, lower, upper, index_of, weights, store):
        @pl.loop(0, count)
        def _(j):
            assemble(None, lower, upper, index_of(j), far_taps)
            gather_columns(0, pl.multiple_of(j * plane, plane))
            gather_columns(edge + 1, pl.multiple_of((count + j) * plane, plane))

        for side in range(2):
            added = jnp.dot(
                cols[side * count * plane : (side + 1) * count * plane, :],
                weights[:, 2 * side * width : (2 * side + 1) * width],
                preferred_element_type=F32,
            )
            for j in range(count):
                total = opened[j, side] + added[j * plane : (j + 1) * plane]
                store(j, side * (edge - 1), jnp.maximum(total, 0.0).astype(BF16))

    def fine_index(b):
        def index(t):
            at = fine_nbr[b, t]
            return jnp.where(at >= 0, at, slots)

        return index

    def take_faces(incoming):
        for s in range(slots):
            below[s] = incoming[0, s].astype(F32).reshape(edge, edge, width)
            above[s] = incoming[1, s].astype(F32).reshape(edge, edge, width)

    loaded(1)
    face = (edge, edge, width)
    cells = half * half

    def pool_copy(k, b):
        if b is None:
            source, at = pooled_out.at[member], slots
        else:
            source, at = pooled.at[member, b], b
        return remote(
            source, source, pool_send_sem.at[k - 1, at], pool_recv_sem.at[k - 1, at], peer(k)
        )

    def pool(value, count):
        pairs = value.reshape(count, 2, half, 2, edge, width)
        summed = (pairs[:, 0, :, 0] + pairs[:, 0, :, 1]) + (pairs[:, 1, :, 0] + pairs[:, 1, :, 1])
        half_z[0 : count * half * edge, :] = summed.reshape(count * half * edge, width)
        even = half_z[pl.ds(0, count * cells, stride=2), :]
        odd = half_z[pl.ds(1, count * cells, stride=2), :]
        return ((even + odd) * 0.125).astype(BF16)

    @pl.loop(0, slots)
    def _(b):
        value = local_product(table, b, fine_index(b), w1).astype(F32)
        value = value.reshape((edge - 2,) + face)
        enc[b, 1 : edge - 1] = value
        pooled[member, b] = pool(value[1 : edge - 3], half - 2)
        for k in range(1, LANES):
            pool_copy(k, b).start()

    finish_pair(halo1[0], has_next, halo1[1], has_prev)
    take_faces(face_in)

    def store_enc(b, x, value):
        enc[b, x] = value.astype(F32).reshape(face)

    outer_planes(slots, below, above, fine_index, w1, store_enc)
    for b in range(slots):
        pooled_out[member, b, 0:cells] = pool(enc[b, 0:2], 1)
        pooled_out[member, b, cells : 2 * cells] = pool(enc[b, edge - 2 : edge], 1)
    for k in range(1, LANES):
        pool_copy(k, None).start()

    for copy in meta_copies:
        copy.wait()
    to_smem = pltpu.make_async_copy(meta, meta_s, meta_sem)
    to_smem.start()
    for k in range(1, LANES):
        for b in (*range(slots), None):
            pool_copy(k, b).wait()
    to_smem.wait()
    for lane in range(LANES):
        for s in range(slots):
            at = lane * slots + s
            children[at, cells : block - cells] = pooled[lane, s].astype(F32)
            children[at, 0:cells] = pooled_out[lane, s, 0:cells].astype(F32)
            children[at, block - cells : block] = pooled_out[lane, s, cells : 2 * cells].astype(F32)

    def owner_of(value):
        value = jnp.maximum(value, 0)
        return lax.div(value, per), lax.rem(value, per)

    @pl.loop(0, bricks)
    def _(j):
        lane, slot = lax.div(j, per), lax.rem(j, per)
        for o in range(8):
            child = meta_s[lane, slot, o]
            safe = jnp.maximum(child, 0)
            at = lax.rem(lax.div(safe, slots), LANES) * slots + lax.rem(safe, slots)
            at = jnp.where(child >= 0, at, LANES * slots)
            ox, oy, oz = o // 4 * half, o // 2 % 2 * half, o % 2 * half
            for x in range(half):
                for y in range(half):
                    row = (x * half + y) * half
                    coarse[j, ox + x, oy + y, oz : oz + half, :] = children[
                        at, row : row + half, :
                    ]

    def side_copies(outgoing, incoming, phase):
        up = remote(
            outgoing,
            incoming.at[0],
            side_send_sem.at[phase, 0],
            side_recv_sem.at[phase, 0],
            me + LANES,
        )
        down = remote(
            outgoing,
            incoming.at[1],
            side_send_sem.at[phase, 1],
            side_recv_sem.at[phase, 1],
            me - LANES,
        )
        return up, down

    def coarse_index(lane, slot, live):
        def index(t):
            value = meta_s[lane, per + slot, t]
            there = (value >= 0) & live
            device, at = owner_of(value)
            at = lax.rem(device, LANES) * per + at
            if t // 9 == 1:
                return jnp.where(there, at, bricks)
            at = at + (lax.div(device, LANES) - group + 1) * bricks
            at = jnp.minimum(jnp.maximum(at, 0), 3 * bricks)
            return jnp.where(there, at, 3 * bricks)

        return index

    def send_sides(source, outgoing, incoming, phase):
        for j in range(bricks):
            first, last = source[j, 0], source[j, edge - 1]
            low_x[bricks + j] = first
            high_x[bricks + j] = last
            outgoing[j, 0] = first.reshape(plane, width).astype(BF16)
            outgoing[j, 1] = last.reshape(plane, width).astype(BF16)
        up, down = side_copies(outgoing, incoming, phase)
        start_pair(up, has_up, down, has_down)
        return up, down

    def take_sides(copies, incoming):
        finish_pair(copies[0], has_up, copies[1], has_down)
        for side, start in ((0, 0), (1, 2 * bricks)):
            for j in range(bricks):
                low_x[start + j] = incoming[side, j, 0].astype(F32).reshape(edge, edge, width)
                high_x[start + j] = incoming[side, j, 1].astype(F32).reshape(edge, edge, width)

    def group_index(j):
        return coarse_index(lax.div(j, per), lax.rem(j, per), True)

    face = (edge, edge, width)
    copies = send_sides(coarse, side_out, side_in, 0)
    loaded(2)

    @pl.loop(0, bricks)
    def _(j):
        value = local_product(coarse, j, group_index(j), w2).astype(F32)
        coarse2[j, 1 : edge - 1] = value.reshape((edge - 2,) + face)

    take_sides(copies, side_in)

    def store_coarse(j, x, value):
        coarse2[j, x] = value.astype(F32).reshape(face)

    outer_planes(bricks, high_x, low_x, group_index, w2, store_coarse)
    copies = send_sides(coarse2, side_out2, side_in2, 1)
    loaded(3)

    part = half * edge
    strip = slots * part

    def quarter(s, taps, planes):
        parent = fine_parent[s]
        safe = jnp.maximum(parent, 0)
        device, slot = owner_of(lax.div(safe, 8))
        octant = lax.rem(safe, 8)
        ox = lax.div(octant, 4) * half
        oy = lax.rem(lax.div(octant, 2), 2) * half
        index = coarse_index(lax.rem(device, LANES), slot, parent >= 0)
        assemble(coarse2, high_x, low_x, index, taps)
        for x in planes:
            start = pl.multiple_of(x * strip + s * part, part)
            for k in range(9):
                dy, dz = k // 3, k % 3 - 1
                piece = pad[ox + x, pl.ds(oy + dy, half), base + dz : base + dz + edge, :]
                cols[pl.ds(start, part), k * width : (k + 1) * width] = piece.reshape(
                    part, width
                ).astype(BF16)

    @pl.loop(0, slots)
    def _(s):
        quarter(s, own_taps, range(1, half + 1))

    take_sides(copies, side_in2)

    @pl.loop(0, slots)
    def _(s):
        quarter(s, range(27), (0, half + 1))

    parents = product(w3, half, strip).astype(F32).reshape(half, slots, part, width)

    for s in range(slots):
        oz = lax.rem(jnp.maximum(fine_parent[s], 0), 2)
        piece = parents[:, s].reshape(half * half * edge, width)
        spread[pl.ds(0, half * half * edge, stride=2), :] = piece
        spread[pl.ds(1, half * half * edge, stride=2), :] = piece
        for z in range(2):
            for row in range(half * half):
                start = row * 2 * edge + z * edge
                lifted[z, row] = spread[start : start + edge, :]
        for x in range(half):
            for y in range(half):
                up = lifted[oz, x * half + y]
                for xx in range(2):
                    for yy in range(2):
                        value = enc[s, 2 * x + xx, 2 * y + yy] + up
                        table[s, 2 * x + xx, 2 * y + yy] = value.astype(BF16).astype(F32)
        stage_faces(face_out2, s)
    halo2 = face_copies(face_out2, face_in2, 1)
    start_pair(halo2[0], has_next, halo2[1], has_prev)
    loaded(4)

    @pl.loop(0, slots)
    def _(b):
        value = local_product(table, b, fine_index(b), w4)
        out_ref[b, plane : (edge - 1) * plane, :] = value

    finish_pair(halo2[0], has_next, halo2[1], has_prev)
    take_faces(face_in2)

    def store_fine(b, x, value):
        out_ref[b, x * plane : (x + 1) * plane, :] = value

    outer_planes(slots, below, above, fine_index, w4, store_fine)


def per_device(
    n,
    features,
    fine_nbr,
    fine_send,
    fine_parent,
    coarse_child,
    coarse_nbr,
    enc_fine_w,
    enc_coarse_w,
    dec_coarse_w,
    dec_fine_w,
):
    slots, edge, width = features.shape[0], features.shape[1], features.shape[-1]
    per = coarse_nbr.shape[0]
    bricks = LANES * per
    half = edge // 2
    plane = edge * edge
    voxels = edge**3
    strip = slots * half * edge
    rows = -(-2 * per // 8) * 8
    kernels = [
        w.reshape(3, 9 * width, width)
        for w in (enc_fine_w, enc_coarse_w, dec_coarse_w, dec_fine_w)
    ]
    vmem = pltpu.VMEM
    smem_spec = pl.BlockSpec(memory_space=pltpu.SMEM)
    vmem_spec = pl.BlockSpec(memory_space=pltpu.VMEM)
    any_spec = pl.BlockSpec(memory_space=pl.ANY)
    cube = (edge, edge, edge, width)
    face = (edge, edge, width)
    dma = pltpu.SemaphoreType.DMA
    out = pl.pallas_call(
        functools.partial(kernel, n),
        out_shape=jax.ShapeDtypeStruct((slots, voxels, width), BF16),
        in_specs=[smem_spec] * 3 + [vmem_spec] * 2 + [any_spec] * 5,
        out_specs=vmem_spec,
        scratch_shapes=[
            vmem((slots, voxels, width), BF16),
            *[vmem((9 * width, 3 * width), BF16)] * 4,
            vmem((edge + 2, edge + 2, 3 * edge, width), F32),
            vmem((max((edge + 2) * plane, (half + 2) * strip, 2 * max(slots, bricks) * plane), 9 * width), BF16),
            vmem((max(slots, bricks), 2, plane, width), F32),
            vmem((slots + 1,) + cube, F32),
            vmem((slots,) + cube, F32),
            vmem((slots + 1,) + face, F32),
            vmem((slots + 1,) + face, F32),
            vmem((2, slots, plane, width), BF16),
            vmem((2, slots, plane, width), BF16),
            vmem((2, slots, plane, width), BF16),
            vmem((2, slots, plane, width), BF16),
            vmem((half * half * edge, width), F32),
            vmem((LANES, slots, (half - 2) * half**2, width), BF16),
            vmem((LANES, slots, 2 * half**2, width), BF16),
            vmem((LANES * slots + 1, half**3, width), F32),
            vmem((LANES, rows, 128), jnp.int32),
            pltpu.SMEM((LANES, rows, 128), jnp.int32),
            vmem((bricks + 1,) + cube, F32),
            vmem((bricks + 1,) + cube, F32),
            vmem((3 * bricks + 1,) + face, F32),
            vmem((3 * bricks + 1,) + face, F32),
            vmem((bricks, 2, plane, width), BF16),
            vmem((2, bricks, 2, plane, width), BF16),
            vmem((bricks, 2, plane, width), BF16),
            vmem((2, bricks, 2, plane, width), BF16),
            vmem((half * half * 2 * edge, width), F32),
            vmem((2, half * half, edge, width), F32),
            dma((5, 3)),
            dma((2, 2)),
            dma((2, 2)),
            dma((LANES - 1, slots + 1)),
            dma((LANES - 1, slots + 1)),
            dma((LANES - 1,)),
            dma((LANES - 1,)),
            dma((2, 2)),
            dma((2, 2)),
            dma(()),
        ],
        compiler_params=pltpu.CompilerParams(
            collective_id=0, has_side_effects=True, vmem_limit_bytes=60 * 1024 * 1024
        ),
    )(
        fine_nbr,
        fine_send[0],
        fine_parent,
        coarse_child,
        coarse_nbr,
        features.reshape(slots, voxels, width),
        *kernels,
    )
    return out.reshape(features.shape)


def solution(mesh):
    lead = ("groups", "gx")
    placed = (
        P(lead, None, None, None, None),
        P(lead, None),
        P(lead, None, None),
        P(lead),
        P(lead, None),
        P(lead, None),
        P(),
        P(),
        P(),
        P(),
    )
    return jax.shard_map(
        functools.partial(per_device, mesh.shape["gx"]),
        mesh=mesh,
        in_specs=placed,
        out_specs=P(lead, None, None, None, None),
        check_vma=False,
    )
```

profile of v0, /device:TPU:0, one launch (start us, length us, event | category | flops | bytes accessed | tf_op | source)
XLA Modules:
  0.0 32.8 jit_solution(11405709841191604001)
XLA Ops:
  0.0 30.9 %shard_map.100 = bf16[4,512,128]{2,1,0:T(8,128)(2,1)} custom-call(s32[4,27]{1,0:T(4,128)} %fine_nbr.1, s32[2,4]{1,0:T(2,128)} %bitcast.13, s32[4]{0:T(128)} %fine_parent.1, s32[1,8]{1,0:T(1,128)} %child_ref.1, s32[1,27]{1,0:T(1,128)} %nbr_ref.1, bf16[4,512,128]{2,1,0:T(8,128)(2,1)} %bitcast.12, bf16[3,1152,128]{2,1,0:T(8,128)(2,1)} %bitcast.8, ...), custom_call_target="tpu_custom_call" | custom-call | tf_op jit(solution)/shard_map/pallas_call | solution.py:564
  30.9 1.9 %copy.12 = bf16[4,8,8,8,128]{4,3,2,1,0:T(8,128)(2,1)} copy(bf16[4,8,8,8,128]{4,3,2,1,0:T(8,128)(2,1)} %bitcast.7) | data formatting | bytes 1048576
where the time goes:
time: 33 us; the launch traced here: 32.8 us
  Pallas kernels  30.9 us (94%)
  local copies, waits for them, and re-layouts  1.87 us (6%)
    pallas_call x1, Pallas kernels, per_device(): pl.pallas_call(functools.partial(kernel, n), out_shape=jax.ShapeDtypeStru...  30.9 us
    unnamed x1, local copies, waits for them, and re-layouts  1.87 us

commit v1 on v0

--- a/solution.py
+++ b/solution.py
@@ -31,17 +31,22 @@
 
 def kernel(
     n,
-    fine_nbr,
-    fine_send,
-    fine_parent,
-    child_ref,
-    nbr_ref,
+    fine_nbr_hbm,
+    fine_send_hbm,
+    fine_parent_hbm,
+    child_hbm,
+    nbr_hbm,
     feat_hbm,
     w1_hbm,
     w2_hbm,
     w3_hbm,
     w4_hbm,
     out_ref,
+    fine_nbr,
+    fine_send,
+    fine_parent,
+    child_ref,
+    nbr_ref,
     feat,
     w1,
     w2,
@@ -75,6 +80,7 @@
     spread,
     lifted,
     load_sem,
+    small_sem,
     face_send_sem,
     face_recv_sem,
     pool_send_sem,
@@ -112,7 +118,23 @@
                 for dx in range(3)
             ]
         )
-    for copies in loads:
+    small = [
+        pltpu.make_async_copy(src, dst, small_sem.at[i])
+        for i, (src, dst) in enumerate(
+            (
+                (fine_nbr_hbm, fine_nbr),
+                (fine_send_hbm, fine_send),
+                (fine_parent_hbm, fine_parent),
+                (child_hbm, child_ref),
+                (nbr_hbm, nbr_ref),
+            )
+        )
+    ]
+    for copy in loads[0]:
+        copy.start()
+    for copy in small:
+        copy.start()
+    for copies in loads[1:]:
         for copy in copies:
             copy.start()
 
@@ -139,7 +161,6 @@
     for there, other in sides:
         pl.when(there)(functools.partial(greet, other))
         peers = peers + jnp.where(there, 1, 0)
-    pl.semaphore_wait(barrier, peers)
 
     def remote(src, dst, send, recv, other):
         return pltpu.make_async_remote_copy(
@@ -183,8 +204,6 @@
             down.wait_recv()
             up.wait_send()
 
-    meta[member, 0:per, 0 : child_ref.shape[1]] = child_ref[...]
-    meta[member, per : 2 * per, 0 : nbr_ref.shape[1]] = nbr_ref[...]
 
     cube = (edge, edge, edge, width)
     zero_brick = jnp.zeros(cube, F32)
@@ -197,13 +216,16 @@
         outgoing[0, s] = table[up_from, edge - 1].reshape(plane, width).astype(BF16)
         outgoing[1, s] = table[down_from, 0].reshape(plane, width).astype(BF16)
 
+    for copy in small:
+        copy.wait()
+    meta[member, 0:per, 0 : child_ref.shape[1]] = child_ref[...]
+    meta[member, per : 2 * per, 0 : nbr_ref.shape[1]] = nbr_ref[...]
     loaded(0)
     for s in range(slots):
         table[s] = feat[s].astype(F32).reshape(cube)
     for s in range(slots):
         stage_faces(face_out, s)
     halo1 = face_copies(face_out, face_in, 0)
-    start_pair(halo1[0], has_next, halo1[1], has_prev)
     meta_copies = [
         remote(
             meta.at[member],
@@ -214,8 +236,6 @@
         )
         for k in range(1, LANES)
     ]
-    for copy in meta_copies:
-        copy.start()
 
     below[slots] = zero_plane
     above[slots] = zero_plane
@@ -334,14 +354,27 @@
         odd = half_z[pl.ds(1, count * cells, stride=2), :]
         return ((even + odd) * 0.125).astype(BF16)
 
-    @pl.loop(0, slots)
-    def _(b):
+    def encode(b):
         value = local_product(table, b, fine_index(b), w1).astype(F32)
         value = value.reshape((edge - 2,) + face)
         enc[b, 1 : edge - 1] = value
         pooled[member, b] = pool(value[1 : edge - 3], half - 2)
+
+    def send_pooled(b):
         for k in range(1, LANES):
             pool_copy(k, b).start()
+
+    encode(0)
+    pl.semaphore_wait(barrier, peers)
+    start_pair(halo1[0], has_next, halo1[1], has_prev)
+    for copy in meta_copies:
+        copy.start()
+    send_pooled(0)
+
+    @pl.loop(1, slots)
+    def _(b):
+        encode(b)
+        send_pooled(b)
 
     finish_pair(halo1[0], has_next, halo1[1], has_prev)
     take_faces(face_in)
@@ -555,7 +588,6 @@
         for w in (enc_fine_w, enc_coarse_w, dec_coarse_w, dec_fine_w)
     ]
     vmem = pltpu.VMEM
-    smem_spec = pl.BlockSpec(memory_space=pltpu.SMEM)
     vmem_spec = pl.BlockSpec(memory_space=pltpu.VMEM)
     any_spec = pl.BlockSpec(memory_space=pl.ANY)
     cube = (edge, edge, edge, width)
@@ -563,10 +595,15 @@
     dma = pltpu.SemaphoreType.DMA
     out = pl.pallas_call(
         functools.partial(kernel, n),
-        out_shape=jax.ShapeDtypeStruct((slots, voxels, width), BF16),
-        in_specs=[smem_spec] * 3 + [vmem_spec] * 2 + [any_spec] * 5,
+        out_shape=pltpu.VMEM((slots, voxels, width), BF16),
+        in_specs=[any_spec] * 10,
         out_specs=vmem_spec,
         scratch_shapes=[
+            pltpu.SMEM(fine_nbr.shape, jnp.int32),
+            pltpu.SMEM(fine_send.shape[1:], jnp.int32),
+            pltpu.SMEM(fine_parent.shape, jnp.int32),
+            vmem(coarse_child.shape, jnp.int32),
+            vmem(coarse_nbr.shape, jnp.int32),
             vmem((slots, voxels, width), BF16),
             *[vmem((9 * width, 3 * width), BF16)] * 4,
             vmem((edge + 2, edge + 2, 3 * edge, width), F32),
@@ -597,6 +634,7 @@
             vmem((half * half * 2 * edge, width), F32),
             vmem((2, half * half, edge, width), F32),
             dma((5, 3)),
+            dma((5,)),
             dma((2, 2)),
             dma((2, 2)),
             dma((LANES - 1, slots + 1)),

time: 33 us -> 30.9 us (0.936)
  local copies, waits for them, and re-layouts: 1.87 us -> 0.8 us
  Pallas kernels: 30.9 us -> 29.9 us
    unnamed x1, local copies, waits for them, and re-layouts: 1.87 us -> 0.8 us
    pallas_call x1, Pallas kernels: 30.9 us -> 29.9 us  [per_device(): pl.pallas_call(functools.partial(kernel, n), out_shape=pltpu.VMEM((slots,...]
where the time goes in v1:
time: 30.9 us; the launch traced here: 30.7 us
  Pallas kernels  29.9 us (97%)
  local copies, waits for them, and re-layouts  0.8 us (3%)
    pallas_call x1, Pallas kernels, per_device(): pl.pallas_call(functools.partial(kernel, n), out_shape=pltpu.VMEM((slots,...  29.9 us
    unnamed x1, local copies, waits for them, and re-layouts  0.8 us

profile of v1, /device:TPU:0, one launch (start us, length us, event | category | flops | bytes accessed | tf_op | source)
XLA Modules:
  0.0 30.7 jit_solution(4341952921602078143)
XLA Ops:
  0.0 29.9 %shard_map.100 = bf16[4,512,128]{2,1,0:T(8,128)(2,1)S(1)} custom-call(s32[4,27]{1,0:T(4,128)} %fine_nbr_hbm.1, s32[2,4]{1,0:T(2,128)} %bitcast.13, s32[4]{0:T(128)} %fine_parent_hbm.1, s32[1,8]{1,0:T(1,128)} %child_hbm.1, s32[1,27]{1,0:T(1,128)} %nbr_hbm.1, bf16[4,512,128]{2,1,0:T(8,128)(2,1)} %bitcast.12, bf16[3,1152,128]{2,1,0:T(8,128)(2,1)} %bitcast.8, ...), custom_call_target="tpu_custom_call" | custom-call | tf_op jit(solution)/shard_map/pallas_call | solution.py:596
  29.9 0.8 %copy.12 = bf16[4,8,8,8,128]{4,3,2,1,0:T(8,128)(2,1)} copy(bf16[4,8,8,8,128]{4,3,2,1,0:T(8,128)(2,1)S(1)} %bitcast.7) | data formatting | bytes 1048576

commit v2 on v1

--- a/solution.py
+++ b/solution.py
@@ -10,6 +10,7 @@
 F32 = jnp.float32
 BF16 = jnp.bfloat16
 LANES = 4
+SPLIT = 2
 MESH = pl.DeviceIdType.MESH
 
 
@@ -52,9 +53,20 @@
     w2,
     w3,
     w4,
+    wup,
     pad,
-    cols,
+    upad,
+    zs,
+    zfar,
+    zq,
+    zu,
     opened,
+    acc,
+    dacc,
+    picks,
+    utab,
+    ubelow,
+    uabove,
     table,
     enc,
     below,
@@ -63,6 +75,8 @@
     face_in,
     face_out2,
     face_in2,
+    face_out3,
+    face_in3,
     half_z,
     pooled,
     pooled_out,
@@ -78,7 +92,6 @@
     side_out2,
     side_in2,
     spread,
-    lifted,
     load_sem,
     small_sem,
     face_send_sem,
@@ -206,15 +219,22 @@
 
 
     cube = (edge, edge, edge, width)
+    face = (edge, edge, width)
+    base = edge
+    padded = (edge + 2) * edge
+    own_taps = range(9, 18)
+    far_taps = (*range(9), *range(18, 27))
     zero_brick = jnp.zeros(cube, F32)
-    zero_plane = jnp.zeros((edge, edge, width), F32)
+    zero_plane = jnp.zeros(face, F32)
     table[slots] = zero_brick
-
-    def stage_faces(outgoing, s):
+    enc[slots] = zero_brick
+
+    def stage_faces(outgoing, source, last, s):
         up_from = jnp.where(fine_send[0, s] >= 0, s, slots)
         down_from = jnp.where(fine_send[1, s] >= 0, s, slots)
-        outgoing[0, s] = table[up_from, edge - 1].reshape(plane, width).astype(BF16)
-        outgoing[1, s] = table[down_from, 0].reshape(plane, width).astype(BF16)
+        rows = outgoing.shape[2]
+        outgoing[0, s] = source[up_from, last].reshape(rows, width).astype(BF16)
+        outgoing[1, s] = source[down_from, 0].reshape(rows, width).astype(BF16)
 
     for copy in small:
         copy.wait()
@@ -224,8 +244,10 @@
     for s in range(slots):
         table[s] = feat[s].astype(F32).reshape(cube)
     for s in range(slots):
-        stage_faces(face_out, s)
+        stage_faces(face_out, table, edge - 1, s)
     halo1 = face_copies(face_out, face_in, 0)
+    halo2 = face_copies(face_out2, face_in2, 1)
+    halo3 = face_copies(face_out3, face_in3, 2)
     meta_copies = [
         remote(
             meta.at[member],
@@ -244,82 +266,81 @@
     low_x[3 * bricks] = zero_plane
     high_x[3 * bricks] = zero_plane
     children[LANES * slots] = jnp.zeros((block, width), F32)
-
-    base = edge
-
-    def assemble(centre, lower, upper, index, taps=range(27)):
+    utab[slots] = jnp.zeros((half, half, edge, width), F32)
+    ubelow[slots] = jnp.zeros((half, edge, width), F32)
+    uabove[slots] = jnp.zeros((half, edge, width), F32)
+
+    def assemble(target, side, centre, lower, upper, index, taps):
         for t in taps:
             dx, dy, dz = t // 9 - 1, t // 3 % 3 - 1, t % 3 - 1
             at = index(t)
-            ys, zs = pick(dy, edge), pick(dz, edge)
+            ys, zs = pick(dy, side), pick(dz, edge)
             if dx == 0:
                 piece = centre[at, :, ys, zs, :]
             elif dx < 0:
                 piece = lower[at, ys, zs, :][None]
             else:
                 piece = upper[at, ys, zs, :][None]
-            pad[place(dx, edge, 1), place(dy, edge, 1), place(dz, edge, base), :] = piece
-
-    def product(weights, planes, rows):
-        two = jnp.dot(
-            cols[0 : (planes + 1) * rows, :],
-            weights[:, 0 : 2 * width],
-            preferred_element_type=F32,
-        )
-        third = jnp.dot(
-            cols[2 * rows : (planes + 2) * rows, :],
-            weights[:, 2 * width : 3 * width],
-            preferred_element_type=F32,
-        )
-        total = third + two[0 : planes * rows, 0:width] + two[rows:, width : 2 * width]
-        return jnp.maximum(total, 0.0).astype(BF16)
-
-    own_taps = range(9, 18)
-    far_taps = (*range(9), *range(18, 27))
-
-    def gather_columns(x, row):
-        for k in range(9):
-            dy, dz = k // 3, k % 3 - 1
-            piece = pad[x, dy : dy + edge, base + dz : base + dz + edge, :]
-            cols[pl.ds(row, plane), k * width : (k + 1) * width] = piece.reshape(
-                plane, width
-            ).astype(BF16)
-
-    def local_product(centre, j, index, weights):
-        assemble(centre, None, None, index, own_taps)
+            target[place(dx, side, 1), place(dy, side, 1), place(dz, edge, base), :] = piece
+
+    def shift(store, row, source, x, y, count):
+        rows = count * edge
+        for dz in range(3):
+            first = base + dz - 1
+            piece = source[x, y, first : first + edge, :]
+            store[dz, pl.ds(row, rows), :] = piece.reshape(rows, width).astype(BF16)
+
+    def columns(store, starts, rows, offsets=(0, 1, 2)):
+        return jnp.concatenate(
+            [
+                jnp.concatenate(
+                    [store[dz, r + dy * edge : r + dy * edge + rows, :] for r in starts], axis=0
+                )
+                for dy in offsets
+                for dz in range(3)
+            ],
+            axis=1,
+        )
+
+    def dot(a, b):
+        return jnp.dot(a, b, preferred_element_type=F32)
+
+    def local_product(centre, index, weights):
+        assemble(pad, edge, centre, None, None, index, own_taps)
+        starts = [x * padded for x in range(edge)]
         for x in range(edge):
-            gather_columns(x + 1, x * plane)
-        two = jnp.dot(
-            cols[0 : edge * plane, :], weights[:, 0 : 2 * width], preferred_element_type=F32
-        )
-        third = jnp.dot(
-            cols[plane : edge * plane, :],
-            weights[:, 2 * width : 3 * width],
-            preferred_element_type=F32,
-        )
-        inner = slice(plane, (edge - 1) * plane)
-        middle = two[:, width : 2 * width]
-        opened[j, 0] = middle[0:plane] + third[0:plane]
-        opened[j, 1] = middle[(edge - 1) * plane :] + two[(edge - 2) * plane : (edge - 1) * plane, 0:width]
-        total = middle[inner] + third[inner] + two[0 : (edge - 2) * plane, 0:width]
-        return jnp.maximum(total, 0.0).astype(BF16)
+            shift(zs, x * padded, pad, x + 1, slice(None), edge + 2)
+        two = dot(columns(zs, starts, plane), weights[:, 0 : 2 * width])
+        third = dot(columns(zs, starts[1:], plane), weights[:, 2 * width : 3 * width])
+        totals = []
+        for x in range(edge):
+            total = two[x * plane : (x + 1) * plane, width : 2 * width]
+            if x > 0:
+                total = total + two[(x - 1) * plane : x * plane, 0:width]
+            if x < edge - 1:
+                total = total + third[x * plane : (x + 1) * plane]
+            totals.append(total)
+        return totals
 
     def outer_planes(count, lower, upper, index_of, weights, store):
         @pl.loop(0, count)
         def _(j):
-            assemble(None, lower, upper, index_of(j), far_taps)
-            gather_columns(0, pl.multiple_of(j * plane, plane))
-            gather_columns(edge + 1, pl.multiple_of((count + j) * plane, plane))
+            assemble(pad, edge, None, lower, upper, index_of(j), far_taps)
+            for side in range(2):
+                row = pl.multiple_of((side * count + j) * padded, edge)
+                shift(zfar, row, pad, side * (edge + 1), slice(None), edge + 2)
 
         for side in range(2):
-            added = jnp.dot(
-                cols[side * count * plane : (side + 1) * count * plane, :],
+            starts = [(side * count + j) * padded for j in range(count)]
+            added = dot(
+                columns(zfar, starts, plane),
                 weights[:, 2 * side * width : (2 * side + 1) * width],
-                preferred_element_type=F32,
             )
             for j in range(count):
-                total = opened[j, side] + added[j * plane : (j + 1) * plane]
-                store(j, side * (edge - 1), jnp.maximum(total, 0.0).astype(BF16))
+                store(j, side, added[j * plane : (j + 1) * plane])
+
+    def rounded(value):
+        return jnp.maximum(value, 0.0).astype(BF16).astype(F32)
 
     def fine_index(b):
         def index(t):
@@ -328,13 +349,12 @@
 
         return index
 
-    def take_faces(incoming):
+    def take_faces(incoming, low, high):
+        shape = low.shape[1:]
         for s in range(slots):
-            below[s] = incoming[0, s].astype(F32).reshape(edge, edge, width)
-            above[s] = incoming[1, s].astype(F32).reshape(edge, edge, width)
-
-    loaded(1)
-    face = (edge, edge, width)
+            low[s] = incoming[0, s].astype(F32).reshape(shape)
+            high[s] = incoming[1, s].astype(F32).reshape(shape)
+
     cells = half * half
 
     def pool_copy(k, b):
@@ -354,8 +374,13 @@
         odd = half_z[pl.ds(1, count * cells, stride=2), :]
         return ((even + odd) * 0.125).astype(BF16)
 
+    loaded(1)
+
     def encode(b):
-        value = local_product(table, b, fine_index(b), w1).astype(F32)
+        totals = local_product(table, fine_index(b), w1)
+        opened[b, 0] = totals[0]
+        opened[b, 1] = totals[edge - 1]
+        value = rounded(jnp.concatenate(totals[1 : edge - 1], axis=0))
         value = value.reshape((edge - 2,) + face)
         enc[b, 1 : edge - 1] = value
         pooled[member, b] = pool(value[1 : edge - 3], half - 2)
@@ -377,10 +402,10 @@
         send_pooled(b)
 
     finish_pair(halo1[0], has_next, halo1[1], has_prev)
-    take_faces(face_in)
-
-    def store_enc(b, x, value):
-        enc[b, x] = value.astype(F32).reshape(face)
+    take_faces(face_in, below, above)
+
+    def store_enc(b, side, added):
+        enc[b, side * (edge - 1)] = rounded(opened[b, side] + added).reshape(face)
 
     outer_planes(slots, below, above, fine_index, w1, store_enc)
     for b in range(slots):
@@ -388,6 +413,42 @@
         pooled_out[member, b, cells : 2 * cells] = pool(enc[b, edge - 2 : edge], 1)
     for k in range(1, LANES):
         pool_copy(k, None).start()
+    for s in range(slots):
+        stage_faces(face_out2, enc, edge - 1, s)
+    start_pair(halo2[0], has_next, halo2[1], has_prev)
+
+    loaded(4)
+
+    def decode_part(b):
+        totals = local_product(enc, fine_index(b), w4)
+        acc[b] = jnp.concatenate(totals, axis=0)
+
+    def run_decode(first, last):
+        @pl.loop(first, last)
+        def _(b):
+            decode_part(b)
+
+    strips = 4
+    span = width // strips
+
+    @pl.loop(0, 3 * strips)
+    def _(i):
+        dz, strip_at = lax.div(i, strips), lax.rem(i, strips)
+        rows = []
+        for dy in range(3):
+            start = pl.multiple_of((dy * 3 + dz) * width + strip_at * span, span)
+            rows.append(w4[pl.ds(start, span), :].astype(F32))
+        for py, parts in enumerate(((rows[0], rows[1] + rows[2]), (rows[0] + rows[1], rows[2]))):
+            for q, part_q in enumerate(parts):
+                a = part_q[:, 0:width]
+                b = part_q[:, width : 2 * width]
+                c = part_q[:, 2 * width : 3 * width]
+                start = pl.multiple_of((q * 3 + dz) * width + strip_at * span, span)
+                wup[py, pl.ds(start, span), :] = jnp.concatenate(
+                    [b + c, a + b, a, c], axis=1
+                ).astype(BF16)
+
+    run_decode(0, SPLIT)
 
     for copy in meta_copies:
         copy.wait()
@@ -470,25 +531,27 @@
         finish_pair(copies[0], has_up, copies[1], has_down)
         for side, start in ((0, 0), (1, 2 * bricks)):
             for j in range(bricks):
-                low_x[start + j] = incoming[side, j, 0].astype(F32).reshape(edge, edge, width)
-                high_x[start + j] = incoming[side, j, 1].astype(F32).reshape(edge, edge, width)
+                low_x[start + j] = incoming[side, j, 0].astype(F32).reshape(face)
+                high_x[start + j] = incoming[side, j, 1].astype(F32).reshape(face)
 
     def group_index(j):
         return coarse_index(lax.div(j, per), lax.rem(j, per), True)
 
-    face = (edge, edge, width)
     copies = send_sides(coarse, side_out, side_in, 0)
     loaded(2)
 
     @pl.loop(0, bricks)
     def _(j):
-        value = local_product(coarse, j, group_index(j), w2).astype(F32)
+        totals = local_product(coarse, group_index(j), w2)
+        opened[j, 0] = totals[0]
+        opened[j, 1] = totals[edge - 1]
+        value = rounded(jnp.concatenate(totals[1 : edge - 1], axis=0))
         coarse2[j, 1 : edge - 1] = value.reshape((edge - 2,) + face)
 
     take_sides(copies, side_in)
 
-    def store_coarse(j, x, value):
-        coarse2[j, x] = value.astype(F32).reshape(face)
+    def store_coarse(j, side, added):
+        coarse2[j, side * (edge - 1)] = rounded(opened[j, side] + added).reshape(face)
 
     outer_planes(bricks, high_x, low_x, group_index, w2, store_coarse)
     copies = send_sides(coarse2, side_out2, side_in2, 1)
@@ -496,70 +559,140 @@
 
     part = half * edge
     strip = slots * part
-
-    def quarter(s, taps, planes):
+    tall = half + 2
+    column = tall * edge
+
+    def parent_of(s):
         parent = fine_parent[s]
         safe = jnp.maximum(parent, 0)
         device, slot = owner_of(lax.div(safe, 8))
         octant = lax.rem(safe, 8)
-        ox = lax.div(octant, 4) * half
-        oy = lax.rem(lax.div(octant, 2), 2) * half
-        index = coarse_index(lax.rem(device, LANES), slot, parent >= 0)
-        assemble(coarse2, high_x, low_x, index, taps)
-        for x in planes:
-            start = pl.multiple_of(x * strip + s * part, part)
-            for k in range(9):
-                dy, dz = k // 3, k % 3 - 1
-                piece = pad[ox + x, pl.ds(oy + dy, half), base + dz : base + dz + edge, :]
-                cols[pl.ds(start, part), k * width : (k + 1) * width] = piece.reshape(
-                    part, width
-                ).astype(BF16)
+        ox, oy = lax.div(octant, 4), lax.rem(lax.div(octant, 2), 2)
+        return coarse_index(lax.rem(device, LANES), slot, parent >= 0), ox, oy * half
+
+    pad[0] = jnp.zeros(pad.shape[1:], F32)
+    pad[edge + 1] = jnp.zeros(pad.shape[1:], F32)
 
     @pl.loop(0, slots)
     def _(s):
-        quarter(s, own_taps, range(1, half + 1))
-
+        index, ox, oy = parent_of(s)
+        assemble(pad, edge, coarse2, None, None, index, own_taps)
+        for x in range(tall):
+            row = pl.multiple_of((s * tall + x) * column, edge)
+            shift(zq, row, pad, ox * half + x, pl.ds(oy, tall), tall)
+
+    def starts_of(planes):
+        return [(s * tall + x) * column for x in planes for s in range(slots)]
+
+    two = dot(columns(zq, starts_of(range(half + 1)), part), w3[:, 0 : 2 * width])
+    third = dot(columns(zq, starts_of(range(2, tall)), part), w3[:, 2 * width : 3 * width])
+    dacc[...] = third + two[0 : half * strip, 0:width] + two[strip:, width : 2 * width]
+
+    run_decode(SPLIT, slots)
+    finish_pair(halo2[0], has_next, halo2[1], has_prev)
+    take_faces(face_in2, below, above)
+
+    def store_part(b, side, added):
+        at = side * (edge - 1) * plane
+        acc[b, at : at + plane] = acc[b, at : at + plane] + added
+
+    outer_planes(slots, below, above, fine_index, w4, store_part)
     take_sides(copies, side_in2)
 
     @pl.loop(0, slots)
     def _(s):
-        quarter(s, range(27), (0, half + 1))
-
-    parents = product(w3, half, strip).astype(F32).reshape(half, slots, part, width)
-
+        index, ox, oy = parent_of(s)
+        assemble(pad, edge, None, high_x, low_x, index, far_taps)
+        row = pl.multiple_of(s * column, edge)
+        shift(zfar, row, pad, ox * (edge + 1), pl.ds(oy, tall), tall)
+
+    far = dot(
+        columns(zfar, [s * column for s in range(slots)], part),
+        jnp.concatenate([w3[:, 0:width], w3[:, 2 * width : 3 * width]], axis=1),
+    )
+    picks[0] = far[:, 0:width]
+    picks[1] = jnp.zeros((strip, width), F32)
+    picks[2] = far[:, width : 2 * width]
     for s in range(slots):
+        _, ox, _ = parent_of(s)
+        rows = slice(s * part, (s + 1) * part)
+        low = picks[ox, rows]
+        high = picks[ox + 1, rows]
+        pieces = [dacc[x * strip + s * part : x * strip + (s + 1) * part, :] for x in range(half)]
+        pieces[0] = pieces[0] + low
+        pieces[half - 1] = pieces[half - 1] + high
+        piece = rounded(jnp.concatenate(pieces, axis=0))
         oz = lax.rem(jnp.maximum(fine_parent[s], 0), 2)
-        piece = parents[:, s].reshape(half * half * edge, width)
-        spread[pl.ds(0, half * half * edge, stride=2), :] = piece
-        spread[pl.ds(1, half * half * edge, stride=2), :] = piece
-        for z in range(2):
-            for row in range(half * half):
-                start = row * 2 * edge + z * edge
-                lifted[z, row] = spread[start : start + edge, :]
+        spread[s, pl.ds(0, half * part, stride=2), :] = piece
+        spread[s, pl.ds(1, half * part, stride=2), :] = piece
         for x in range(half):
             for y in range(half):
-                up = lifted[oz, x * half + y]
-                for xx in range(2):
-                    for yy in range(2):
-                        value = enc[s, 2 * x + xx, 2 * y + yy] + up
-                        table[s, 2 * x + xx, 2 * y + yy] = value.astype(BF16).astype(F32)
-        stage_faces(face_out2, s)
-    halo2 = face_copies(face_out2, face_in2, 1)
-    start_pair(halo2[0], has_next, halo2[1], has_prev)
-    loaded(4)
+                start = ((x * half + y) * 2 + oz) * edge
+                utab[s, x, y] = spread[s, pl.ds(start, edge), :]
+        stage_faces(face_out3, utab, half - 1, s)
+    start_pair(halo3[0], has_next, halo3[1], has_prev)
+
+    brick_rows = tall * column
 
     @pl.loop(0, slots)
     def _(b):
-        value = local_product(table, b, fine_index(b), w4)
-        out_ref[b, plane : (edge - 1) * plane, :] = value
-
-    finish_pair(halo2[0], has_next, halo2[1], has_prev)
-    take_faces(face_in2)
-
-    def store_fine(b, x, value):
-        out_ref[b, x * plane : (x + 1) * plane, :] = value
-
-    outer_planes(slots, below, above, fine_index, w4, store_fine)
+        assemble(upad, half, utab, None, None, fine_index(b), own_taps)
+        for x in range(half):
+            row = pl.multiple_of(b * brick_rows + (x + 1) * column, edge)
+            shift(zu, row, upad, x + 1, slice(None), tall)
+
+    def woven(zero, one):
+        pair = jnp.stack(
+            [zero.reshape(half, edge, width), one.reshape(half, edge, width)], axis=1
+        )
+        return pair.reshape(plane, width)
+
+    inner = [b * brick_rows + (x + 1) * column for b in range(slots) for x in range(half)]
+    direct, across = [], []
+    for py in range(2):
+        lhs = columns(zu, inner, part, (py, py + 1))
+        direct.append(dot(lhs, wup[py, :, 0 : 2 * width]))
+        across.append(dot(columns(zu, inner, part, (py, py + 1)), wup[py, :, 2 * width :]))
+
+    for b in range(slots):
+        for x in range(edge):
+            i, px = x // 2, x % 2
+            lanes = slice(px * width, (px + 1) * width)
+            other = i - 1 + 2 * px
+            sums = []
+            for py in range(2):
+                at = (b * half + i) * part
+                value = direct[py][at : at + part, lanes]
+                if 0 <= other < half:
+                    at = (b * half + other) * part
+                    value = value + across[py][at : at + part, lanes]
+                sums.append(value)
+            rows = slice(x * plane, (x + 1) * plane)
+            total = acc[b, rows] + woven(*sums)
+            if 0 <= other < half:
+                out_ref[b, rows, :] = jnp.maximum(total, 0.0).astype(BF16)
+            else:
+                acc[b, rows] = total
+
+    finish_pair(halo3[0], has_next, halo3[1], has_prev)
+    take_faces(face_in3, ubelow, uabove)
+
+    @pl.loop(0, slots)
+    def _(b):
+        assemble(upad, half, None, ubelow, uabove, fine_index(b), far_taps)
+        for x in (0, half + 1):
+            row = pl.multiple_of(b * brick_rows + x * column, edge)
+            shift(zu, row, upad, x, slice(None), tall)
+
+    for side in range(2):
+        starts = [b * brick_rows + side * (half + 1) * column for b in range(slots)]
+        lanes = slice((2 + side) * width, (3 + side) * width)
+        sums = [dot(columns(zu, starts, part, (py, py + 1)), wup[py, :, lanes]) for py in range(2)]
+        for b in range(slots):
+            at = side * (edge - 1) * plane
+            rows = slice(b * part, (b + 1) * part)
+            total = acc[b, at : at + plane] + woven(sums[0][rows], sums[1][rows])
+            out_ref[b, at : at + plane, :] = jnp.maximum(total, 0.0).astype(BF16)
 
 
 def per_device(
@@ -581,7 +714,8 @@
     half = edge // 2
     plane = edge * edge
     voxels = edge**3
-    strip = slots * half * edge
+    padded = (edge + 2) * edge
+    tall = half + 2
     rows = -(-2 * per // 8) * 8
     kernels = [
         w.reshape(3, 9 * width, width)
@@ -606,17 +740,30 @@
             vmem(coarse_nbr.shape, jnp.int32),
             vmem((slots, voxels, width), BF16),
             *[vmem((9 * width, 3 * width), BF16)] * 4,
+            vmem((2, 6 * width, 4 * width), BF16),
             vmem((edge + 2, edge + 2, 3 * edge, width), F32),
-            vmem((max((edge + 2) * plane, (half + 2) * strip, 2 * max(slots, bricks) * plane), 9 * width), BF16),
+            vmem((half + 2, half + 2, 3 * edge, width), F32),
+            vmem((3, edge * padded, width), BF16),
+            vmem((3, 2 * max(slots, bricks) * padded, width), BF16),
+            vmem((3, slots * tall * tall * edge, width), BF16),
+            vmem((3, slots * tall * tall * edge, width), BF16),
             vmem((max(slots, bricks), 2, plane, width), F32),
+            vmem((slots, voxels, width), F32),
+            vmem((half * slots * half * edge, width), F32),
+            vmem((3, slots * half * edge, width), F32),
+            vmem((slots + 1, half, half, edge, width), F32),
+            vmem((slots + 1, half, edge, width), F32),
+            vmem((slots + 1, half, edge, width), F32),
             vmem((slots + 1,) + cube, F32),
-            vmem((slots,) + cube, F32),
+            vmem((slots + 1,) + cube, F32),
             vmem((slots + 1,) + face, F32),
             vmem((slots + 1,) + face, F32),
             vmem((2, slots, plane, width), BF16),
             vmem((2, slots, plane, width), BF16),
             vmem((2, slots, plane, width), BF16),
             vmem((2, slots, plane, width), BF16),
+            vmem((2, slots, half * edge, width), BF16),
+            vmem((2, slots, half * edge, width), BF16),
             vmem((half * half * edge, width), F32),
             vmem((LANES, slots, (half - 2) * half**2, width), BF16),
             vmem((LANES, slots, 2 * half**2, width), BF16),
@@ -631,12 +778,11 @@
             vmem((2, bricks, 2, plane, width), BF16),
             vmem((bricks, 2, plane, width), BF16),
             vmem((2, bricks, 2, plane, width), BF16),
-            vmem((half * half * 2 * edge, width), F32),
-            vmem((2, half * half, edge, width), F32),
+            vmem((slots, half * half * 2 * edge, width), F32),
             dma((5, 3)),
             dma((5,)),
-            dma((2, 2)),
-            dma((2, 2)),
+            dma((3, 2)),
+            dma((3, 2)),
             dma((LANES - 1, slots + 1)),
             dma((LANES - 1, slots + 1)),
             dma((LANES - 1,)),

time: 30.9 us -> 28.8 us (0.932)
  the two profiles are of different devices: /device:TPU:0 before, /device:TPU:5 now
where the time goes in v2:
time: 28.8 us; the launch traced here: 28.4 us
  Pallas kernels  27.6 us (96%)
  local copies, waits for them, and re-layouts  0.8 us (3%)
    pallas_call x1, Pallas kernels, per_device(): pl.pallas_call(functools.partial(kernel, n), out_shape=pltpu.VMEM((slots,...  27.6 us
    unnamed x1, local copies, waits for them, and re-layouts  0.8 us

profile of v2, /device:TPU:5, one launch (start us, length us, event | category | flops | bytes accessed | tf_op | source)
XLA Modules:
  0.0 28.4 jit_solution(124156636942838068)
XLA Ops:
  0.0 27.6 %shard_map.100 = bf16[4,512,128]{2,1,0:T(8,128)(2,1)S(1)} custom-call(s32[4,27]{1,0:T(4,128)} %fine_nbr_hbm.1, s32[2,4]{1,0:T(2,128)} %bitcast.13, s32[4]{0:T(128)} %fine_parent_hbm.1, s32[1,8]{1,0:T(1,128)} %child_hbm.1, s32[1,27]{1,0:T(1,128)} %nbr_hbm.1, bf16[4,512,128]{2,1,0:T(8,128)(2,1)} %bitcast.12, bf16[3,1152,128]{2,1,0:T(8,128)(2,1)} %bitcast.8, ...), custom_call_target="tpu_custom_call" | custom-call | tf_op jit(solution)/shard_map/pallas_call | solution.py:730
  27.6 0.8 %copy.12 = bf16[4,8,8,8,128]{4,3,2,1,0:T(8,128)(2,1)} copy(bf16[4,8,8,8,128]{4,3,2,1,0:T(8,128)(2,1)S(1)} %bitcast.7) | data formatting | bytes 1048576

commit v3 on v2

--- a/solution.py
+++ b/solution.py
@@ -37,6 +37,7 @@
     fine_parent_hbm,
     child_hbm,
     nbr_hbm,
+    parent_row_hbm,
     feat_hbm,
     w1_hbm,
     w2_hbm,
@@ -48,6 +49,7 @@
     fine_parent,
     child_ref,
     nbr_ref,
+    parent_row,
     feat,
     w1,
     w2,
@@ -83,6 +85,9 @@
     children,
     meta,
     meta_s,
+    meta_far,
+    meta_far_s,
+    far_children,
     coarse,
     coarse2,
     low_x,
@@ -103,6 +108,7 @@
     side_send_sem,
     side_recv_sem,
     meta_sem,
+    far_sem,
 ):
     slots, edge = out_ref.shape[0], enc.shape[1]
     plane = edge * edge
@@ -119,18 +125,11 @@
         return me - member + (member ^ k)
 
     width = out_ref.shape[-1]
-    loads = [[pltpu.make_async_copy(feat_hbm, feat, load_sem.at[0, 0])]]
+    loads = [[pltpu.make_async_copy(feat_hbm, feat, load_sem.at[0])]]
     for i, (src, dst) in enumerate(
         ((w1_hbm, w1), (w2_hbm, w2), (w3_hbm, w3), (w4_hbm, w4))
     ):
-        loads.append(
-            [
-                pltpu.make_async_copy(
-                    src.at[dx], dst.at[:, dx * width : (dx + 1) * width], load_sem.at[i + 1, dx]
-                )
-                for dx in range(3)
-            ]
-        )
+        loads.append([pltpu.make_async_copy(src, dst, load_sem.at[i + 1])])
     small = [
         pltpu.make_async_copy(src, dst, small_sem.at[i])
         for i, (src, dst) in enumerate(
@@ -140,6 +139,7 @@
                 (fine_parent_hbm, fine_parent),
                 (child_hbm, child_ref),
                 (nbr_hbm, nbr_ref),
+                (parent_row_hbm, parent_row),
             )
         )
     ]
@@ -236,13 +236,14 @@
         outgoing[0, s] = source[up_from, last].reshape(rows, width).astype(BF16)
         outgoing[1, s] = source[down_from, 0].reshape(rows, width).astype(BF16)
 
+    loaded(0)
+    for s in range(slots):
+        table[s] = feat[s].astype(F32).reshape(cube)
     for copy in small:
         copy.wait()
     meta[member, 0:per, 0 : child_ref.shape[1]] = child_ref[...]
     meta[member, per : 2 * per, 0 : nbr_ref.shape[1]] = nbr_ref[...]
-    loaded(0)
-    for s in range(slots):
-        table[s] = feat[s].astype(F32).reshape(cube)
+    meta[member, 2 * per : 2 * per + 1, 0:slots] = parent_row[...]
     for s in range(slots):
         stage_faces(face_out, table, edge - 1, s)
     halo1 = face_copies(face_out, face_in, 0)
@@ -302,23 +303,42 @@
             axis=1,
         )
 
+    def taps(weights, *sides):
+        return jnp.concatenate([weights[dx] for dx in sides], axis=1)
+
     def dot(a, b):
         return jnp.dot(a, b, preferred_element_type=F32)
+
+    def stepped(store, start, rows, weight):
+        third = 3 * width
+        first, middle, last = (weight[i * third : (i + 1) * third, :] for i in range(3))
+        both = jnp.concatenate(
+            [
+                jnp.concatenate([first, middle], axis=1),
+                jnp.concatenate([jnp.zeros((third, width), BF16), last], axis=1),
+            ],
+            axis=0,
+        )
+        return dot(columns(store, [start], rows, (0, 1)), both)
+
+    def tread(value, at):
+        row = at * padded
+        return value[row : row + plane, 0:width] + value[row + edge : row + edge + plane, width:]
 
     def local_product(centre, index, weights):
         assemble(pad, edge, centre, None, None, index, own_taps)
         starts = [x * padded for x in range(edge)]
         for x in range(edge):
             shift(zs, x * padded, pad, x + 1, slice(None), edge + 2)
-        two = dot(columns(zs, starts, plane), weights[:, 0 : 2 * width])
-        third = dot(columns(zs, starts[1:], plane), weights[:, 2 * width : 3 * width])
+        two = dot(columns(zs, starts, plane), taps(weights, 0, 1))
+        third = stepped(zs, padded, (edge - 1) * padded, weights[2])
         totals = []
         for x in range(edge):
             total = two[x * plane : (x + 1) * plane, width : 2 * width]
             if x > 0:
                 total = total + two[(x - 1) * plane : x * plane, 0:width]
             if x < edge - 1:
-                total = total + third[x * plane : (x + 1) * plane]
+                total = total + tread(third, x)
             totals.append(total)
         return totals
 
@@ -331,13 +351,9 @@
                 shift(zfar, row, pad, side * (edge + 1), slice(None), edge + 2)
 
         for side in range(2):
-            starts = [(side * count + j) * padded for j in range(count)]
-            added = dot(
-                columns(zfar, starts, plane),
-                weights[:, 2 * side * width : (2 * side + 1) * width],
-            )
+            added = stepped(zfar, side * count * padded, count * padded, weights[2 * side])
             for j in range(count):
-                store(j, side, added[j * plane : (j + 1) * plane])
+                store(j, side, tread(added, j))
 
     def rounded(value):
         return jnp.maximum(value, 0.0).astype(BF16).astype(F32)
@@ -374,6 +390,27 @@
         odd = half_z[pl.ds(1, count * cells, stride=2), :]
         return ((even + odd) * 0.125).astype(BF16)
 
+    def side_copies(outgoing, incoming, phase):
+        up = remote(
+            outgoing,
+            incoming.at[0],
+            side_send_sem.at[phase, 0],
+            side_recv_sem.at[phase, 0],
+            me + LANES,
+        )
+        down = remote(
+            outgoing,
+            incoming.at[1],
+            side_send_sem.at[phase, 1],
+            side_recv_sem.at[phase, 1],
+            me - LANES,
+        )
+        return up, down
+
+    pl.semaphore_wait(barrier, peers)
+    for copy in meta_copies:
+        copy.start()
+    start_pair(halo1[0], has_next, halo1[1], has_prev)
     loaded(1)
 
     def encode(b):
@@ -390,10 +427,6 @@
             pool_copy(k, b).start()
 
     encode(0)
-    pl.semaphore_wait(barrier, peers)
-    start_pair(halo1[0], has_next, halo1[1], has_prev)
-    for copy in meta_copies:
-        copy.start()
     send_pooled(0)
 
     @pl.loop(1, slots)
@@ -404,18 +437,23 @@
     finish_pair(halo1[0], has_next, halo1[1], has_prev)
     take_faces(face_in, below, above)
 
+    for copy in meta_copies:
+        copy.wait()
+    to_smem = pltpu.make_async_copy(meta, meta_s, meta_sem)
+    to_smem.start()
+    hop_meta = side_copies(meta, meta_far, 2)
+    start_pair(hop_meta[0], has_up, hop_meta[1], has_down)
     def store_enc(b, side, added):
         enc[b, side * (edge - 1)] = rounded(opened[b, side] + added).reshape(face)
 
     outer_planes(slots, below, above, fine_index, w1, store_enc)
     for b in range(slots):
-        pooled_out[member, b, 0:cells] = pool(enc[b, 0:2], 1)
-        pooled_out[member, b, cells : 2 * cells] = pool(enc[b, edge - 2 : edge], 1)
+        pooled_out[member, b, 0] = pool(enc[b, 0:2], 1)
+        pooled_out[member, b, 1] = pool(enc[b, edge - 2 : edge], 1)
     for k in range(1, LANES):
         pool_copy(k, None).start()
     for s in range(slots):
         stage_faces(face_out2, enc, edge - 1, s)
-    start_pair(halo2[0], has_next, halo2[1], has_prev)
 
     loaded(4)
 
@@ -437,12 +475,11 @@
         rows = []
         for dy in range(3):
             start = pl.multiple_of((dy * 3 + dz) * width + strip_at * span, span)
-            rows.append(w4[pl.ds(start, span), :].astype(F32))
-        for py, parts in enumerate(((rows[0], rows[1] + rows[2]), (rows[0] + rows[1], rows[2]))):
-            for q, part_q in enumerate(parts):
-                a = part_q[:, 0:width]
-                b = part_q[:, width : 2 * width]
-                c = part_q[:, 2 * width : 3 * width]
+            rows.append([w4[dx, pl.ds(start, span), :].astype(F32) for dx in range(3)])
+        late = [r1 + r2 for r1, r2 in zip(rows[1], rows[2])]
+        early = [r0 + r1 for r0, r1 in zip(rows[0], rows[1])]
+        for py, parts in enumerate(((rows[0], late), (early, rows[2]))):
+            for q, (a, b, c) in enumerate(parts):
                 start = pl.multiple_of((q * 3 + dz) * width + strip_at * span, span)
                 wup[py, pl.ds(start, span), :] = jnp.concatenate(
                     [b + c, a + b, a, c], axis=1
@@ -450,20 +487,35 @@
 
     run_decode(0, SPLIT)
 
-    for copy in meta_copies:
-        copy.wait()
-    to_smem = pltpu.make_async_copy(meta, meta_s, meta_sem)
-    to_smem.start()
+    to_smem.wait()
+    finish_pair(hop_meta[0], has_up, hop_meta[1], has_down)
+
+    def far_to_smem(side):
+        return pltpu.make_async_copy(meta_far.at[side], meta_far_s.at[side], far_sem.at[side])
+
+    pl.when(has_down)(lambda: far_to_smem(0).start())
+    pl.when(has_up)(lambda: far_to_smem(1).start())
     for k in range(1, LANES):
         for b in (*range(slots), None):
             pool_copy(k, b).wait()
-    to_smem.wait()
+    for lane in range(LANES):
+        for s in range(slots):
+            octant = lax.rem(jnp.maximum(meta_s[lane, 2 * per, s], 0), 8)
+            side_out[lane * slots + s] = pooled_out[lane, s, lax.div(octant, 4)]
+    copies = side_copies(side_out, side_in, 0)
+    start_pair(copies[0], has_up, copies[1], has_down)
+    start_pair(halo2[0], has_next, halo2[1], has_prev)
     for lane in range(LANES):
         for s in range(slots):
             at = lane * slots + s
             children[at, cells : block - cells] = pooled[lane, s].astype(F32)
-            children[at, 0:cells] = pooled_out[lane, s, 0:cells].astype(F32)
-            children[at, block - cells : block] = pooled_out[lane, s, cells : 2 * cells].astype(F32)
+            children[at, 0:cells] = pooled_out[lane, s, 0].astype(F32)
+            children[at, block - cells : block] = pooled_out[lane, s, 1].astype(F32)
+
+    def child_at(child):
+        safe = jnp.maximum(child, 0)
+        at = lax.rem(lax.div(safe, slots), LANES) * slots + lax.rem(safe, slots)
+        return jnp.where(child >= 0, at, LANES * slots)
 
     def owner_of(value):
         value = jnp.maximum(value, 0)
@@ -473,10 +525,7 @@
     def _(j):
         lane, slot = lax.div(j, per), lax.rem(j, per)
         for o in range(8):
-            child = meta_s[lane, slot, o]
-            safe = jnp.maximum(child, 0)
-            at = lax.rem(lax.div(safe, slots), LANES) * slots + lax.rem(safe, slots)
-            at = jnp.where(child >= 0, at, LANES * slots)
+            at = child_at(meta_s[lane, slot, o])
             ox, oy, oz = o // 4 * half, o // 2 % 2 * half, o % 2 * half
             for x in range(half):
                 for y in range(half):
@@ -484,23 +533,6 @@
                     coarse[j, ox + x, oy + y, oz : oz + half, :] = children[
                         at, row : row + half, :
                     ]
-
-    def side_copies(outgoing, incoming, phase):
-        up = remote(
-            outgoing,
-            incoming.at[0],
-            side_send_sem.at[phase, 0],
-            side_recv_sem.at[phase, 0],
-            me + LANES,
-        )
-        down = remote(
-            outgoing,
-            incoming.at[1],
-            side_send_sem.at[phase, 1],
-            side_recv_sem.at[phase, 1],
-            me - LANES,
-        )
-        return up, down
 
     def coarse_index(lane, slot, live):
         def index(t):
@@ -516,16 +548,37 @@
 
         return index
 
+    def keep_sides(source):
+        for j in range(bricks):
+            low_x[bricks + j] = source[j, 0]
+            high_x[bricks + j] = source[j, edge - 1]
+
     def send_sides(source, outgoing, incoming, phase):
         for j in range(bricks):
-            first, last = source[j, 0], source[j, edge - 1]
-            low_x[bricks + j] = first
-            high_x[bricks + j] = last
-            outgoing[j, 0] = first.reshape(plane, width).astype(BF16)
-            outgoing[j, 1] = last.reshape(plane, width).astype(BF16)
+            outgoing[j, 0] = source[j, 0].reshape(plane, width).astype(BF16)
+            outgoing[j, 1] = source[j, edge - 1].reshape(plane, width).astype(BF16)
         up, down = side_copies(outgoing, incoming, phase)
         start_pair(up, has_up, down, has_down)
+        keep_sides(source)
         return up, down
+
+    def place_far(side):
+        start = 2 * bricks * side
+        for at in range(LANES * slots):
+            far_children[side, at] = side_in[side, at].astype(F32)
+        far_children[side, LANES * slots] = jnp.zeros((cells, width), F32)
+
+        @pl.loop(0, bricks)
+        def _(j):
+            lane, slot = lax.div(j, per), lax.rem(j, per)
+            for o in range(8):
+                at = child_at(meta_far_s[side, lane, slot, o])
+                oy, oz = o // 2 % 2 * half, o % 2 * half
+                target = high_x if o // 4 else low_x
+                for y in range(half):
+                    target[start + j, oy + y, oz : oz + half, :] = far_children[
+                        side, at, y * half : (y + 1) * half, :
+                    ]
 
     def take_sides(copies, incoming):
         finish_pair(copies[0], has_up, copies[1], has_down)
@@ -537,7 +590,7 @@
     def group_index(j):
         return coarse_index(lax.div(j, per), lax.rem(j, per), True)
 
-    copies = send_sides(coarse, side_out, side_in, 0)
+    keep_sides(coarse)
     loaded(2)
 
     @pl.loop(0, bricks)
@@ -548,7 +601,11 @@
         value = rounded(jnp.concatenate(totals[1 : edge - 1], axis=0))
         coarse2[j, 1 : edge - 1] = value.reshape((edge - 2,) + face)
 
-    take_sides(copies, side_in)
+    finish_pair(copies[0], has_up, copies[1], has_down)
+    pl.when(has_down)(lambda: far_to_smem(0).wait())
+    pl.when(has_up)(lambda: far_to_smem(1).wait())
+    pl.when(has_down)(lambda: place_far(0))
+    pl.when(has_up)(lambda: place_far(1))
 
     def store_coarse(j, side, added):
         coarse2[j, side * (edge - 1)] = rounded(opened[j, side] + added).reshape(face)
@@ -584,8 +641,8 @@
     def starts_of(planes):
         return [(s * tall + x) * column for x in planes for s in range(slots)]
 
-    two = dot(columns(zq, starts_of(range(half + 1)), part), w3[:, 0 : 2 * width])
-    third = dot(columns(zq, starts_of(range(2, tall)), part), w3[:, 2 * width : 3 * width])
+    two = dot(columns(zq, starts_of(range(half + 1)), part), taps(w3, 0, 1))
+    third = dot(columns(zq, starts_of(range(2, tall)), part), w3[2])
     dacc[...] = third + two[0 : half * strip, 0:width] + two[strip:, width : 2 * width]
 
     run_decode(SPLIT, slots)
@@ -608,7 +665,7 @@
 
     far = dot(
         columns(zfar, [s * column for s in range(slots)], part),
-        jnp.concatenate([w3[:, 0:width], w3[:, 2 * width : 3 * width]], axis=1),
+        taps(w3, 0, 2),
     )
     picks[0] = far[:, 0:width]
     picks[1] = jnp.zeros((strip, width), F32)
@@ -716,7 +773,7 @@
     voxels = edge**3
     padded = (edge + 2) * edge
     tall = half + 2
-    rows = -(-2 * per // 8) * 8
+    rows = -(-(2 * per + 1) // 8) * 8
     kernels = [
         w.reshape(3, 9 * width, width)
         for w in (enc_fine_w, enc_coarse_w, dec_coarse_w, dec_fine_w)
@@ -730,7 +787,7 @@
     out = pl.pallas_call(
         functools.partial(kernel, n),
         out_shape=pltpu.VMEM((slots, voxels, width), BF16),
-        in_specs=[any_spec] * 10,
+        in_specs=[any_spec] * 11,
         out_specs=vmem_spec,
         scratch_shapes=[
             pltpu.SMEM(fine_nbr.shape, jnp.int32),
@@ -738,13 +795,14 @@
             pltpu.SMEM(fine_parent.shape, jnp.int32),
             vmem(coarse_child.shape, jnp.int32),
             vmem(coarse_nbr.shape, jnp.int32),
+            vmem((1,) + fine_parent.shape, jnp.int32),
             vmem((slots, voxels, width), BF16),
-            *[vmem((9 * width, 3 * width), BF16)] * 4,
+            *[vmem((3, 9 * width, width), BF16)] * 4,
             vmem((2, 6 * width, 4 * width), BF16),
             vmem((edge + 2, edge + 2, 3 * edge, width), F32),
             vmem((half + 2, half + 2, 3 * edge, width), F32),
-            vmem((3, edge * padded, width), BF16),
-            vmem((3, 2 * max(slots, bricks) * padded, width), BF16),
+            vmem((3, edge * padded + edge, width), BF16),
+            vmem((3, 2 * max(slots, bricks) * padded + edge, width), BF16),
             vmem((3, slots * tall * tall * edge, width), BF16),
             vmem((3, slots * tall * tall * edge, width), BF16),
             vmem((max(slots, bricks), 2, plane, width), F32),
@@ -766,30 +824,34 @@
             vmem((2, slots, half * edge, width), BF16),
             vmem((half * half * edge, width), F32),
             vmem((LANES, slots, (half - 2) * half**2, width), BF16),
-            vmem((LANES, slots, 2 * half**2, width), BF16),
+            vmem((LANES, slots, 2, half**2, width), BF16),
             vmem((LANES * slots + 1, half**3, width), F32),
             vmem((LANES, rows, 128), jnp.int32),
             pltpu.SMEM((LANES, rows, 128), jnp.int32),
+            vmem((2, LANES, rows, 128), jnp.int32),
+            pltpu.SMEM((2, LANES, rows, 128), jnp.int32),
+            vmem((2, LANES * slots + 1, half**2, width), F32),
             vmem((bricks + 1,) + cube, F32),
             vmem((bricks + 1,) + cube, F32),
             vmem((3 * bricks + 1,) + face, F32),
             vmem((3 * bricks + 1,) + face, F32),
-            vmem((bricks, 2, plane, width), BF16),
-            vmem((2, bricks, 2, plane, width), BF16),
+            vmem((LANES * slots, half**2, width), BF16),
+            vmem((2, LANES * slots, half**2, width), BF16),
             vmem((bricks, 2, plane, width), BF16),
             vmem((2, bricks, 2, plane, width), BF16),
             vmem((slots, half * half * 2 * edge, width), F32),
-            dma((5, 3)),
             dma((5,)),
+            dma((6,)),
             dma((3, 2)),
             dma((3, 2)),
             dma((LANES - 1, slots + 1)),
             dma((LANES - 1, slots + 1)),
             dma((LANES - 1,)),
             dma((LANES - 1,)),
-            dma((2, 2)),
-            dma((2, 2)),
+            dma((3, 2)),
+            dma((3, 2)),
             dma(()),
+            dma((2,)),
         ],
         compiler_params=pltpu.CompilerParams(
             collective_id=0, has_side_effects=True, vmem_limit_bytes=60 * 1024 * 1024
@@ -800,6 +862,7 @@
         fine_parent,
         coarse_child,
         coarse_nbr,
+        fine_parent[None],
         features.reshape(slots, voxels, width),
         *kernels,
     )

time: 28.8 us -> 26.4 us (0.917)
  Pallas kernels: 27.6 us -> 25.4 us
    pallas_call x1, Pallas kernels: 27.6 us -> 25.4 us  [per_device(): pl.pallas_call(functools.partial(kernel, n), out_shape=pltpu.VMEM((slots,...]
where the time goes in v3:
time: 26.4 us; the launch traced here: 26.2 us
  Pallas kernels  25.4 us (96%)
  local copies, waits for them, and re-layouts  0.8 us (3%)
    pallas_call x1, Pallas kernels, per_device(): pl.pallas_call(functools.partial(kernel, n), out_shape=pltpu.VMEM((slots,...  25.4 us
    unnamed x1, local copies, waits for them, and re-layouts  0.8 us

profile of v3, /device:TPU:5, one launch (start us, length us, event | category | flops | bytes accessed | tf_op | source)
XLA Modules:
  0.0 26.2 jit_solution(11584382398326062914)
XLA Ops:
  0.0 25.4 %shard_map.100 = bf16[4,512,128]{2,1,0:T(8,128)(2,1)S(1)} custom-call(s32[4,27]{1,0:T(4,128)} %fine_nbr_hbm.1, s32[2,4]{1,0:T(2,128)} %bitcast.15, s32[4]{0:T(128)} %fine_parent_hbm.1, s32[1,8]{1,0:T(1,128)} %child_hbm.1, s32[1,27]{1,0:T(1,128)} %nbr_hbm.1, s32[1,4]{1,0:T(1,128)} %bitcast.14, bf16[4,512,128]{2,1,0:T(8,128)(2,1)} %bitcast.13, ...), custom_call_target="tpu_custom_call" | custom-call | tf_op jit(solution)/shard_map/pallas_call | solution.py:787
  25.4 0.8 %copy.12 = bf16[4,8,8,8,128]{4,3,2,1,0:T(8,128)(2,1)} copy(bf16[4,8,8,8,128]{4,3,2,1,0:T(8,128)(2,1)S(1)} %bitcast.8) | data formatting | bytes 1048576

commit v4 on v3

--- a/solution.py
+++ b/solution.py
@@ -10,7 +10,6 @@
 F32 = jnp.float32
 BF16 = jnp.bfloat16
 LANES = 4
-SPLIT = 2
 MESH = pl.DeviceIdType.MESH
 
 
@@ -37,7 +36,6 @@
     fine_parent_hbm,
     child_hbm,
     nbr_hbm,
-    parent_row_hbm,
     feat_hbm,
     w1_hbm,
     w2_hbm,
@@ -49,7 +47,6 @@
     fine_parent,
     child_ref,
     nbr_ref,
-    parent_row,
     feat,
     w1,
     w2,
@@ -82,6 +79,7 @@
     half_z,
     pooled,
     pooled_out,
+    own_out,
     children,
     meta,
     meta_s,
@@ -96,6 +94,9 @@
     side_in,
     side_out2,
     side_in2,
+    outer_in,
+    inner_out,
+    inner_in,
     spread,
     load_sem,
     small_sem,
@@ -107,6 +108,9 @@
     meta_recv_sem,
     side_send_sem,
     side_recv_sem,
+    pair_send_sem,
+    pair_recv_sem,
+    ready_sem,
     meta_sem,
     far_sem,
 ):
@@ -139,7 +143,6 @@
                 (fine_parent_hbm, fine_parent),
                 (child_hbm, child_ref),
                 (nbr_hbm, nbr_ref),
-                (parent_row_hbm, parent_row),
             )
         )
     ]
@@ -162,14 +165,15 @@
     def greet(other):
         pl.semaphore_signal(barrier, inc=1, device_id={"gx": other}, device_id_type=MESH)
 
+    for k in range(1, LANES):
+        greet(peer(k))
+    first = me - member
     sides = (
         (has_prev & (member == 0), me - 1),
         (has_next & (member == LANES - 1), me + 1),
         (has_down, me - LANES),
         (has_up, me + LANES),
     )
-    for k in range(1, LANES):
-        greet(peer(k))
     peers = LANES - 1
     for there, other in sides:
         pl.when(there)(functools.partial(greet, other))
@@ -243,7 +247,6 @@
         copy.wait()
     meta[member, 0:per, 0 : child_ref.shape[1]] = child_ref[...]
     meta[member, per : 2 * per, 0 : nbr_ref.shape[1]] = nbr_ref[...]
-    meta[member, 2 * per : 2 * per + 1, 0:slots] = parent_row[...]
     for s in range(slots):
         stage_faces(face_out, table, edge - 1, s)
     halo1 = face_copies(face_out, face_in, 0)
@@ -253,8 +256,8 @@
         remote(
             meta.at[member],
             meta.at[member],
-            meta_send_sem.at[k - 1],
-            meta_recv_sem.at[k - 1],
+            meta_send_sem,
+            meta_recv_sem,
             peer(k),
         )
         for k in range(1, LANES)
@@ -309,7 +312,7 @@
     def dot(a, b):
         return jnp.dot(a, b, preferred_element_type=F32)
 
-    def stepped(store, start, rows, weight):
+    def stepped(store, starts, rows, weight):
         third = 3 * width
         first, middle, last = (weight[i * third : (i + 1) * third, :] for i in range(3))
         both = jnp.concatenate(
@@ -319,11 +322,10 @@
             ],
             axis=0,
         )
-        return dot(columns(store, [start], rows, (0, 1)), both)
-
-    def tread(value, at):
-        row = at * padded
-        return value[row : row + plane, 0:width] + value[row + edge : row + edge + plane, width:]
+        return dot(columns(store, starts, rows, (0, 1)), both)
+
+    def tread(value, row, rows):
+        return value[row : row + rows, 0:width] + value[row + edge : row + edge + rows, width:]
 
     def local_product(centre, index, weights):
         assemble(pad, edge, centre, None, None, index, own_taps)
@@ -331,14 +333,14 @@
         for x in range(edge):
             shift(zs, x * padded, pad, x + 1, slice(None), edge + 2)
         two = dot(columns(zs, starts, plane), taps(weights, 0, 1))
-        third = stepped(zs, padded, (edge - 1) * padded, weights[2])
+        third = stepped(zs, [padded], (edge - 1) * padded, weights[2])
         totals = []
         for x in range(edge):
             total = two[x * plane : (x + 1) * plane, width : 2 * width]
             if x > 0:
                 total = total + two[(x - 1) * plane : x * plane, 0:width]
             if x < edge - 1:
-                total = total + tread(third, x)
+                total = total + tread(third, x * padded, plane)
             totals.append(total)
         return totals
 
@@ -351,9 +353,9 @@
                 shift(zfar, row, pad, side * (edge + 1), slice(None), edge + 2)
 
         for side in range(2):
-            added = stepped(zfar, side * count * padded, count * padded, weights[2 * side])
+            added = stepped(zfar, [side * count * padded], count * padded, weights[2 * side])
             for j in range(count):
-                store(j, side, tread(added, j))
+                store(j, side, tread(added, j * padded, plane))
 
     def rounded(value):
         return jnp.maximum(value, 0.0).astype(BF16).astype(F32)
@@ -374,12 +376,16 @@
     cells = half * half
 
     def pool_copy(k, b):
-        if b is None:
-            source, at = pooled_out.at[member], slots
-        else:
-            source, at = pooled.at[member, b], b
+        source = pooled_out.at[member] if b is None else pooled.at[member, b]
+        stage = int(b is None)
         return remote(
-            source, source, pool_send_sem.at[k - 1, at], pool_recv_sem.at[k - 1, at], peer(k)
+            source, source, pool_send_sem.at[stage], pool_recv_sem.at[stage], peer(k)
+        )
+
+    def all_pooled(stage):
+        source = (pooled, pooled_out)[stage].at[0 : LANES - 1]
+        return remote(
+            source, source, pool_send_sem.at[stage], pool_recv_sem.at[stage], peer(1)
         )
 
     def pool(value, count):
@@ -408,6 +414,8 @@
         return up, down
 
     pl.semaphore_wait(barrier, peers)
+    for k in range(1, LANES):
+        pl.semaphore_signal(ready_sem, inc=1, device_id={"gx": peer(k)}, device_id_type=MESH)
     for copy in meta_copies:
         copy.start()
     start_pair(halo1[0], has_next, halo1[1], has_prev)
@@ -426,10 +434,8 @@
         for k in range(1, LANES):
             pool_copy(k, b).start()
 
-    encode(0)
-    send_pooled(0)
-
-    @pl.loop(1, slots)
+
+    @pl.loop(0, slots)
     def _(b):
         encode(b)
         send_pooled(b)
@@ -437,8 +443,8 @@
     finish_pair(halo1[0], has_next, halo1[1], has_prev)
     take_faces(face_in, below, above)
 
-    for copy in meta_copies:
-        copy.wait()
+    every_meta = meta.at[0 : LANES - 1]
+    remote(every_meta, every_meta, meta_send_sem, meta_recv_sem, peer(1)).wait()
     to_smem = pltpu.make_async_copy(meta, meta_s, meta_sem)
     to_smem.start()
     hop_meta = side_copies(meta, meta_far, 2)
@@ -448,10 +454,33 @@
 
     outer_planes(slots, below, above, fine_index, w1, store_enc)
     for b in range(slots):
-        pooled_out[member, b, 0] = pool(enc[b, 0:2], 1)
-        pooled_out[member, b, 1] = pool(enc[b, edge - 2 : edge], 1)
+        for side in range(2):
+            start = side * (edge - 2)
+            value = pool(enc[b, start : start + 2], 1)
+            pooled_out[member, b, side] = value
+            own_out[b, side] = value
     for k in range(1, LANES):
         pool_copy(k, None).start()
+    for s in range(slots):
+        octant = lax.rem(jnp.maximum(fine_parent[s], 0), 8)
+        side_out[s] = own_out[s, lax.div(octant, 4)]
+
+    def face_to(side, lane):
+        return remote(
+            side_out,
+            side_in.at[side, member],
+            side_send_sem.at[0, side],
+            side_recv_sem.at[0, side],
+            first + (LANES if side == 0 else -LANES) + lane,
+        )
+
+    def faces_to(side):
+        for lane in range(LANES):
+            face_to(side, lane).start()
+
+    pl.semaphore_wait(ready_sem, LANES - 1)
+    pl.when(has_up)(lambda: faces_to(0))
+    pl.when(has_down)(lambda: faces_to(1))
     for s in range(slots):
         stage_faces(face_out2, enc, edge - 1, s)
 
@@ -485,7 +514,7 @@
                     [b + c, a + b, a, c], axis=1
                 ).astype(BF16)
 
-    run_decode(0, SPLIT)
+    run_decode(0, slots)
 
     to_smem.wait()
     finish_pair(hop_meta[0], has_up, hop_meta[1], has_down)
@@ -495,15 +524,8 @@
 
     pl.when(has_down)(lambda: far_to_smem(0).start())
     pl.when(has_up)(lambda: far_to_smem(1).start())
-    for k in range(1, LANES):
-        for b in (*range(slots), None):
-            pool_copy(k, b).wait()
-    for lane in range(LANES):
-        for s in range(slots):
-            octant = lax.rem(jnp.maximum(meta_s[lane, 2 * per, s], 0), 8)
-            side_out[lane * slots + s] = pooled_out[lane, s, lax.div(octant, 4)]
-    copies = side_copies(side_out, side_in, 0)
-    start_pair(copies[0], has_up, copies[1], has_down)
+    for stage in range(2):
+        all_pooled(stage).wait()
     start_pair(halo2[0], has_next, halo2[1], has_prev)
     for lane in range(LANES):
         for s in range(slots):
@@ -553,19 +575,17 @@
             low_x[bricks + j] = source[j, 0]
             high_x[bricks + j] = source[j, edge - 1]
 
-    def send_sides(source, outgoing, incoming, phase):
-        for j in range(bricks):
-            outgoing[j, 0] = source[j, 0].reshape(plane, width).astype(BF16)
-            outgoing[j, 1] = source[j, edge - 1].reshape(plane, width).astype(BF16)
-        up, down = side_copies(outgoing, incoming, phase)
-        start_pair(up, has_up, down, has_down)
-        keep_sides(source)
-        return up, down
+    own = bricks // 2
+    parity = lax.rem(member, 2)
+
+    def brick_of(i, odd):
+        return (2 * lax.div(i, per) + odd) * per + lax.rem(i, per)
 
     def place_far(side):
         start = 2 * bricks * side
-        for at in range(LANES * slots):
-            far_children[side, at] = side_in[side, at].astype(F32)
+        for lane in range(LANES):
+            for s in range(slots):
+                far_children[side, lane * slots + s] = side_in[side, lane, s].astype(F32)
         far_children[side, LANES * slots] = jnp.zeros((cells, width), F32)
 
         @pl.loop(0, bricks)
@@ -580,38 +600,91 @@
                         side, at, y * half : (y + 1) * half, :
                     ]
 
-    def take_sides(copies, incoming):
-        finish_pair(copies[0], has_up, copies[1], has_down)
-        for side, start in ((0, 0), (1, 2 * bricks)):
-            for j in range(bricks):
-                low_x[start + j] = incoming[side, j, 0].astype(F32).reshape(face)
-                high_x[start + j] = incoming[side, j, 1].astype(F32).reshape(face)
-
     def group_index(j):
         return coarse_index(lax.div(j, per), lax.rem(j, per), True)
 
     keep_sides(coarse)
     loaded(2)
 
-    @pl.loop(0, bricks)
-    def _(j):
-        totals = local_product(coarse, group_index(j), w2)
-        opened[j, 0] = totals[0]
-        opened[j, 1] = totals[edge - 1]
-        value = rounded(jnp.concatenate(totals[1 : edge - 1], axis=0))
-        coarse2[j, 1 : edge - 1] = value.reshape((edge - 2,) + face)
-
-    finish_pair(copies[0], has_up, copies[1], has_down)
+    def own_index(i):
+        return group_index(brick_of(i, parity))
+
+    def inner_copy(i):
+        return remote(
+            inner_out.at[i], inner_in.at[i], pair_send_sem.at[0], pair_recv_sem.at[0], peer(1)
+        )
+
+    @pl.loop(0, own)
+    def _(i):
+        totals = local_product(coarse, own_index(i), w2)
+        opened[i, 0] = totals[0]
+        opened[i, 1] = totals[edge - 1]
+        value = jnp.maximum(jnp.concatenate(totals[1 : edge - 1], axis=0), 0.0).astype(BF16)
+        inner_out[i] = value
+        coarse2[brick_of(i, parity), 1 : edge - 1] = value.astype(F32).reshape(
+            (edge - 2,) + face
+        )
+        inner_copy(i).start()
+
+    def all_faces(side):
+        return remote(
+            side_in.at[side],
+            side_in.at[side],
+            side_send_sem.at[0, side],
+            side_recv_sem.at[0, side],
+            me + (LANES if side == 0 else -LANES),
+        )
+
+    @pl.when(has_down)
+    def _():
+        all_faces(0).wait_recv()
+        all_faces(1).wait_send()
+
+    @pl.when(has_up)
+    def _():
+        all_faces(1).wait_recv()
+        all_faces(0).wait_send()
+
     pl.when(has_down)(lambda: far_to_smem(0).wait())
     pl.when(has_up)(lambda: far_to_smem(1).wait())
     pl.when(has_down)(lambda: place_far(0))
     pl.when(has_up)(lambda: place_far(1))
 
-    def store_coarse(j, side, added):
-        coarse2[j, side * (edge - 1)] = rounded(opened[j, side] + added).reshape(face)
-
-    outer_planes(bricks, high_x, low_x, group_index, w2, store_coarse)
-    copies = send_sides(coarse2, side_out2, side_in2, 1)
+    def store_coarse(i, side, added):
+        value = jnp.maximum(opened[i, side] + added, 0.0).astype(BF16)
+        side_out2[i, side] = value
+        coarse2[brick_of(i, parity), side * (edge - 1)] = value.astype(F32).reshape(face)
+
+    outer_planes(own, high_x, low_x, own_index, w2, store_coarse)
+
+    def planes_to(side, k):
+        return remote(
+            side_out2,
+            side_in2.at[side, parity],
+            side_send_sem.at[1, side],
+            side_recv_sem.at[1, side],
+            peer(k) + (LANES if side == 0 else -LANES),
+        )
+
+    def all_planes(side):
+        return remote(
+            side_in2.at[side],
+            side_in2.at[side],
+            side_send_sem.at[1, side],
+            side_recv_sem.at[1, side],
+            me + (LANES if side == 0 else -LANES),
+        )
+
+    def send_planes(side):
+        for k in range(2):
+            planes_to(side, k).start()
+
+    pl.when(has_up)(lambda: send_planes(0))
+    pl.when(has_down)(lambda: send_planes(1))
+    outer_copy = remote(
+        side_out2, outer_in, pair_send_sem.at[1], pair_recv_sem.at[1], peer(1)
+    )
+    outer_copy.start()
     loaded(3)
 
     part = half * edge
@@ -627,6 +700,14 @@
         ox, oy = lax.div(octant, 4), lax.rem(lax.div(octant, 2), 2)
         return coarse_index(lax.rem(device, LANES), slot, parent >= 0), ox, oy * half
 
+    remote(inner_out, inner_in, pair_send_sem.at[0], pair_recv_sem.at[0], peer(1)).wait()
+    outer_copy.wait()
+    for i in range(own):
+        at = brick_of(i, 1 - parity)
+        coarse2[at, 1 : edge - 1] = inner_in[i].astype(F32).reshape((edge - 2,) + face)
+        coarse2[at, 0] = outer_in[i, 0].astype(F32).reshape(face)
+        coarse2[at, edge - 1] = outer_in[i, 1].astype(F32).reshape(face)
+    keep_sides(coarse2)
     pad[0] = jnp.zeros(pad.shape[1:], F32)
     pad[edge + 1] = jnp.zeros(pad.shape[1:], F32)
 
@@ -642,10 +723,18 @@
         return [(s * tall + x) * column for x in planes for s in range(slots)]
 
     two = dot(columns(zq, starts_of(range(half + 1)), part), taps(w3, 0, 1))
-    third = dot(columns(zq, starts_of(range(2, tall)), part), w3[2])
-    dacc[...] = third + two[0 : half * strip, 0:width] + two[strip:, width : 2 * width]
-
-    run_decode(SPLIT, slots)
+    third = stepped(
+        zq, [(s * tall + 2) * column for s in range(slots)], half * column, w3[2]
+    )
+    for x in range(half):
+        for s in range(slots):
+            at = x * strip + s * part
+            dacc[at : at + part, :] = (
+                two[at : at + part, 0:width]
+                + two[at + strip : at + strip + part, width : 2 * width]
+                + tread(third, (s * half + x) * column, part)
+            )
+
     finish_pair(halo2[0], has_next, halo2[1], has_prev)
     take_faces(face_in2, below, above)
 
@@ -654,7 +743,23 @@
         acc[b, at : at + plane] = acc[b, at : at + plane] + added
 
     outer_planes(slots, below, above, fine_index, w4, store_part)
-    take_sides(copies, side_in2)
+    @pl.when(has_down)
+    def _():
+        all_planes(0).wait_recv()
+        all_planes(1).wait_send()
+
+    @pl.when(has_up)
+    def _():
+        all_planes(1).wait_recv()
+        all_planes(0).wait_send()
+
+    for side in range(2):
+        for odd in range(2):
+            for i in range(own):
+                at = 2 * bricks * side + (2 * (i // per) + odd) * per + i % per
+                low_x[at] = side_in2[side, odd, i, 0].astype(F32).reshape(face)
+                high_x[at] = side_in2[side, odd, i, 1].astype(F32).reshape(face)
+
 
     @pl.loop(0, slots)
     def _(s):
@@ -773,7 +878,7 @@
     voxels = edge**3
     padded = (edge + 2) * edge
     tall = half + 2
-    rows = -(-(2 * per + 1) // 8) * 8
+    rows = -(-2 * per // 8) * 8
     kernels = [
         w.reshape(3, 9 * width, width)
         for w in (enc_fine_w, enc_coarse_w, dec_coarse_w, dec_fine_w)
@@ -787,7 +892,7 @@
     out = pl.pallas_call(
         functools.partial(kernel, n),
         out_shape=pltpu.VMEM((slots, voxels, width), BF16),
-        in_specs=[any_spec] * 11,
+        in_specs=[any_spec] * 10,
         out_specs=vmem_spec,
         scratch_shapes=[
             pltpu.SMEM(fine_nbr.shape, jnp.int32),
@@ -795,7 +900,6 @@
             pltpu.SMEM(fine_parent.shape, jnp.int32),
             vmem(coarse_child.shape, jnp.int32),
             vmem(coarse_nbr.shape, jnp.int32),
-            vmem((1,) + fine_parent.shape, jnp.int32),
             vmem((slots, voxels, width), BF16),
             *[vmem((3, 9 * width, width), BF16)] * 4,
             vmem((2, 6 * width, 4 * width), BF16),
@@ -803,7 +907,7 @@
             vmem((half + 2, half + 2, 3 * edge, width), F32),
             vmem((3, edge * padded + edge, width), BF16),
             vmem((3, 2 * max(slots, bricks) * padded + edge, width), BF16),
-            vmem((3, slots * tall * tall * edge, width), BF16),
+            vmem((3, slots * tall * tall * edge + edge, width), BF16),
             vmem((3, slots * tall * tall * edge, width), BF16),
             vmem((max(slots, bricks), 2, plane, width), F32),
             vmem((slots, voxels, width), F32),
@@ -825,6 +929,7 @@
             vmem((half * half * edge, width), F32),
             vmem((LANES, slots, (half - 2) * half**2, width), BF16),
             vmem((LANES, slots, 2, half**2, width), BF16),
+            vmem((slots, 2, half**2, width), BF16),
             vmem((LANES * slots + 1, half**3, width), F32),
             vmem((LANES, rows, 128), jnp.int32),
             pltpu.SMEM((LANES, rows, 128), jnp.int32),
@@ -835,21 +940,27 @@
             vmem((bricks + 1,) + cube, F32),
             vmem((3 * bricks + 1,) + face, F32),
             vmem((3 * bricks + 1,) + face, F32),
-            vmem((LANES * slots, half**2, width), BF16),
-            vmem((2, LANES * slots, half**2, width), BF16),
-            vmem((bricks, 2, plane, width), BF16),
-            vmem((2, bricks, 2, plane, width), BF16),
+            vmem((slots, half**2, width), BF16),
+            vmem((2, LANES, slots, half**2, width), BF16),
+            vmem((bricks // 2, 2, plane, width), BF16),
+            vmem((2, 2, bricks // 2, 2, plane, width), BF16),
+            vmem((bricks // 2, 2, plane, width), BF16),
+            vmem((bricks // 2, (edge - 2) * plane, width), BF16),
+            vmem((bricks // 2, (edge - 2) * plane, width), BF16),
             vmem((slots, half * half * 2 * edge, width), F32),
             dma((5,)),
-            dma((6,)),
+            dma((5,)),
             dma((3, 2)),
             dma((3, 2)),
-            dma((LANES - 1, slots + 1)),
-            dma((LANES - 1, slots + 1)),
-            dma((LANES - 1,)),
-            dma((LANES - 1,)),
+            dma((2,)),
+            dma((2,)),
+            dma(()),
+            dma(()),
             dma((3, 2)),
             dma((3, 2)),
+            dma((2,)),
+            dma((2,)),
+            pltpu.SemaphoreType.REGULAR,
             dma(()),
             dma((2,)),
         ],
@@ -862,7 +973,6 @@
         fine_parent,
         coarse_child,
         coarse_nbr,
-        fine_parent[None],
         features.reshape(slots, voxels, width),
         *kernels,
     )

time: 26.4 us -> 25.2 us (0.955)
  Pallas kernels: 25.4 us -> 24.1 us
    pallas_call x1, Pallas kernels: 25.4 us -> 24.1 us  [per_device(): pl.pallas_call(functools.partial(kernel, n), out_shape=pltpu.VMEM((slots,...]
where the time goes in v4:
time: 25.2 us; the launch traced here: 24.9 us
  Pallas kernels  24.1 us (96%)
  local copies, waits for them, and re-layouts  0.8 us (3%)
    pallas_call x1, Pallas kernels, per_device(): pl.pallas_call(functools.partial(kernel, n), out_shape=pltpu.VMEM((slots,...  24.1 us
    unnamed x1, local copies, waits for them, and re-layouts  0.8 us

profile of v4, /device:TPU:5, one launch (start us, length us, event | category | flops | bytes accessed | tf_op | source)
XLA Modules:
  0.0 24.9 jit_solution(9441104969874587418)
XLA Ops:
  0.0 24.1 %shard_map.100 = bf16[4,512,128]{2,1,0:T(8,128)(2,1)S(1)} custom-call(s32[4,27]{1,0:T(4,128)} %fine_nbr_hbm.1, s32[2,4]{1,0:T(2,128)} %bitcast.13, s32[4]{0:T(128)} %fine_parent_hbm.1, s32[1,8]{1,0:T(1,128)} %child_hbm.1, s32[1,27]{1,0:T(1,128)} %nbr_hbm.1, bf16[4,512,128]{2,1,0:T(8,128)(2,1)} %bitcast.12, bf16[3,1152,128]{2,1,0:T(8,128)(2,1)} %bitcast.8, ...), custom_call_target="tpu_custom_call" | custom-call | tf_op jit(solution)/shard_map/pallas_call | solution.py:892
  24.1 0.8 %copy.12 = bf16[4,8,8,8,128]{4,3,2,1,0:T(8,128)(2,1)} copy(bf16[4,8,8,8,128]{4,3,2,1,0:T(8,128)(2,1)S(1)} %bitcast.7) | data formatting | bytes 1048576

commit v5 on v4

--- a/solution.py
+++ b/solution.py
@@ -94,9 +94,8 @@
     side_in,
     side_out2,
     side_in2,
-    outer_in,
-    inner_out,
-    inner_in,
+    brick_out,
+    brick_in,
     spread,
     load_sem,
     small_sem,
@@ -479,8 +478,6 @@
             face_to(side, lane).start()
 
     pl.semaphore_wait(ready_sem, LANES - 1)
-    pl.when(has_up)(lambda: faces_to(0))
-    pl.when(has_down)(lambda: faces_to(1))
     for s in range(slots):
         stage_faces(face_out2, enc, edge - 1, s)
 
@@ -494,6 +491,189 @@
         @pl.loop(first, last)
         def _(b):
             decode_part(b)
+
+            @pl.when(b == 0)
+            def _():
+                pl.when(has_up)(lambda: faces_to(0))
+                pl.when(has_down)(lambda: faces_to(1))
+
+    run_decode(0, slots)
+
+    to_smem.wait()
+    finish_pair(hop_meta[0], has_up, hop_meta[1], has_down)
+
+    def far_to_smem(side):
+        return pltpu.make_async_copy(meta_far.at[side], meta_far_s.at[side], far_sem.at[side])
+
+    pl.when(has_down)(lambda: far_to_smem(0).start())
+    pl.when(has_up)(lambda: far_to_smem(1).start())
+    for stage in range(2):
+        all_pooled(stage).wait()
+    start_pair(halo2[0], has_next, halo2[1], has_prev)
+    for lane in range(LANES):
+        for s in range(slots):
+            at = lane * slots + s
+            children[at, cells : block - cells] = pooled[lane, s].astype(F32)
+            children[at, 0:cells] = pooled_out[lane, s, 0].astype(F32)
+            children[at, block - cells : block] = pooled_out[lane, s, 1].astype(F32)
+
+    def child_at(child, start):
+        at = jnp.clip(child - start * LANES * slots, 0, LANES * slots - 1)
+        return jnp.where(child >= 0, at, LANES * slots)
+
+    def halves(value, size):
+        if size == 1:
+            return value, 0
+        return lax.div(value, size), lax.rem(value, size)
+
+    @pl.loop(0, bricks)
+    def _(j):
+        lane, slot = halves(j, per)
+        for o in range(8):
+            at = child_at(meta_s[lane, slot, o], group)
+            ox, oy, oz = o // 4 * half, o // 2 % 2 * half, o % 2 * half
+            for x in range(half):
+                for y in range(half):
+                    row = (x * half + y) * half
+                    coarse[j, ox + x, oy + y, oz : oz + half, :] = children[
+                        at, row : row + half, :
+                    ]
+
+    def coarse_index(lane, slot, live):
+        def index(t):
+            value = meta_s[lane, per + slot, t]
+            there = (value >= 0) & live
+            if t // 9 == 1:
+                return jnp.where(there, jnp.clip(value - group * bricks, 0, bricks - 1), bricks)
+            at = jnp.clip(value - (group - 1) * bricks, 0, 3 * bricks - 1)
+            return jnp.where(there, at, 3 * bricks)
+
+        return index
+
+    def keep_sides(source):
+        for j in range(bricks):
+            low_x[bricks + j] = source[j, 0]
+            high_x[bricks + j] = source[j, edge - 1]
+
+    own = bricks // 2
+    parity = lax.rem(member, 2)
+
+    def brick_of(i, odd):
+        lane, slot = halves(i, per)
+        return (2 * lane + odd) * per + slot
+
+    def place_far(side):
+        start = 2 * bricks * side
+        for lane in range(LANES):
+            for s in range(slots):
+                far_children[side, lane * slots + s] = side_in[side, lane, s].astype(F32)
+        far_children[side, LANES * slots] = jnp.zeros((cells, width), F32)
+
+        @pl.loop(0, bricks)
+        def _(j):
+            lane, slot = halves(j, per)
+            for o in range(8):
+                at = child_at(meta_far_s[side, lane, slot, o], group - 1 + 2 * side)
+                oy, oz = o // 2 % 2 * half, o % 2 * half
+                target = high_x if o // 4 else low_x
+                for y in range(half):
+                    target[start + j, oy + y, oz : oz + half, :] = far_children[
+                        side, at, y * half : (y + 1) * half, :
+                    ]
+
+    def group_index(j):
+        return coarse_index(*halves(j, per), True)
+
+    keep_sides(coarse)
+    def all_faces(side):
+        return remote(
+            side_in.at[side],
+            side_in.at[side],
+            side_send_sem.at[0, side],
+            side_recv_sem.at[0, side],
+            me + (LANES if side == 0 else -LANES),
+        )
+
+    @pl.when(has_down)
+    def _():
+        all_faces(0).wait_recv()
+        all_faces(1).wait_send()
+
+    @pl.when(has_up)
+    def _():
+        all_faces(1).wait_recv()
+        all_faces(0).wait_send()
+
+    pl.when(has_down)(lambda: far_to_smem(0).wait())
+    pl.when(has_up)(lambda: far_to_smem(1).wait())
+    pl.when(has_down)(lambda: place_far(0))
+    pl.when(has_up)(lambda: place_far(1))
+
+    loaded(2)
+
+    def own_index(i):
+        return group_index(brick_of(i, parity))
+
+    def brick_copy(i):
+        return remote(brick_out.at[i], brick_in.at[i], pair_send_sem, pair_recv_sem, peer(1))
+
+    def planes_to(side, i, k):
+        return remote(
+            side_out2.at[i],
+            side_in2.at[side, parity, i],
+            side_send_sem.at[1, side],
+            side_recv_sem.at[1, side],
+            peer(k) + (LANES if side == 0 else -LANES),
+        )
+
+    def all_planes(side):
+        return remote(
+            side_in2.at[side],
+            side_in2.at[side],
+            side_send_sem.at[1, side],
+            side_recv_sem.at[1, side],
+            me + (LANES if side == 0 else -LANES),
+        )
+
+    @pl.loop(0, own)
+    def _(i):
+        index = own_index(i)
+        totals = local_product(coarse, index, w2)
+        assemble(pad, edge, None, high_x, low_x, index, far_taps)
+        for side in range(2):
+            shift(zfar, side * padded, pad, side * (edge + 1), slice(None), edge + 2)
+        for side in range(2):
+            added = stepped(zfar, [side * padded], padded, w2[2 * side])
+            at = side * (edge - 1)
+            totals[at] = totals[at] + tread(added, 0, plane)
+        value = jnp.maximum(jnp.concatenate(totals, axis=0), 0.0).astype(BF16)
+        side_out2[i, 0] = value[0:plane]
+        side_out2[i, 1] = value[(edge - 1) * plane :]
+        brick_out[i] = value
+        coarse2[brick_of(i, parity)] = value.astype(F32).reshape(cube)
+
+        def send_planes(side):
+            for k in range(2):
+                planes_to(side, i, k).start()
+
+        pl.when(has_up)(lambda: send_planes(0))
+        pl.when(has_down)(lambda: send_planes(1))
+        brick_copy(i).start()
+
+    loaded(3)
+
+    part = half * edge
+    strip = slots * part
+    tall = half + 2
+    column = tall * edge
+
+    def parent_of(s):
+        parent = fine_parent[s]
+        safe = jnp.maximum(parent, 0)
+        lane, slot = halves(jnp.clip(safe // 8 - group * bricks, 0, bricks - 1), per)
+        octant = safe % 8
+        ox, oy = lax.div(octant, 4), lax.rem(lax.div(octant, 2), 2)
+        return coarse_index(lane, slot, parent >= 0), ox, oy * half
 
     strips = 4
     span = width // strips
@@ -514,199 +694,9 @@
                     [b + c, a + b, a, c], axis=1
                 ).astype(BF16)
 
-    run_decode(0, slots)
-
-    to_smem.wait()
-    finish_pair(hop_meta[0], has_up, hop_meta[1], has_down)
-
-    def far_to_smem(side):
-        return pltpu.make_async_copy(meta_far.at[side], meta_far_s.at[side], far_sem.at[side])
-
-    pl.when(has_down)(lambda: far_to_smem(0).start())
-    pl.when(has_up)(lambda: far_to_smem(1).start())
-    for stage in range(2):
-        all_pooled(stage).wait()
-    start_pair(halo2[0], has_next, halo2[1], has_prev)
-    for lane in range(LANES):
-        for s in range(slots):
-            at = lane * slots + s
-            children[at, cells : block - cells] = pooled[lane, s].astype(F32)
-            children[at, 0:cells] = pooled_out[lane, s, 0].astype(F32)
-            children[at, block - cells : block] = pooled_out[lane, s, 1].astype(F32)
-
-    def child_at(child):
-        safe = jnp.maximum(child, 0)
-        at = lax.rem(lax.div(safe, slots), LANES) * slots + lax.rem(safe, slots)
-        return jnp.where(child >= 0, at, LANES * slots)
-
-    def owner_of(value):
-        value = jnp.maximum(value, 0)
-        return lax.div(value, per), lax.rem(value, per)
-
-    @pl.loop(0, bricks)
-    def _(j):
-        lane, slot = lax.div(j, per), lax.rem(j, per)
-        for o in range(8):
-            at = child_at(meta_s[lane, slot, o])
-            ox, oy, oz = o // 4 * half, o // 2 % 2 * half, o % 2 * half
-            for x in range(half):
-                for y in range(half):
-                    row = (x * half + y) * half
-                    coarse[j, ox + x, oy + y, oz : oz + half, :] = children[
-                        at, row : row + half, :
-                    ]
-
-    def coarse_index(lane, slot, live):
-        def index(t):
-            value = meta_s[lane, per + slot, t]
-            there = (value >= 0) & live
-            device, at = owner_of(value)
-            at = lax.rem(device, LANES) * per + at
-            if t // 9 == 1:
-                return jnp.where(there, at, bricks)
-            at = at + (lax.div(device, LANES) - group + 1) * bricks
-            at = jnp.minimum(jnp.maximum(at, 0), 3 * bricks)
-            return jnp.where(there, at, 3 * bricks)
-
-        return index
-
-    def keep_sides(source):
-        for j in range(bricks):
-            low_x[bricks + j] = source[j, 0]
-            high_x[bricks + j] = source[j, edge - 1]
-
-    own = bricks // 2
-    parity = lax.rem(member, 2)
-
-    def brick_of(i, odd):
-        return (2 * lax.div(i, per) + odd) * per + lax.rem(i, per)
-
-    def place_far(side):
-        start = 2 * bricks * side
-        for lane in range(LANES):
-            for s in range(slots):
-                far_children[side, lane * slots + s] = side_in[side, lane, s].astype(F32)
-        far_children[side, LANES * slots] = jnp.zeros((cells, width), F32)
-
-        @pl.loop(0, bricks)
-        def _(j):
-            lane, slot = lax.div(j, per), lax.rem(j, per)
-            for o in range(8):
-                at = child_at(meta_far_s[side, lane, slot, o])
-                oy, oz = o // 2 % 2 * half, o % 2 * half
-                target = high_x if o // 4 else low_x
-                for y in range(half):
-                    target[start + j, oy + y, oz : oz + half, :] = far_children[
-                        side, at, y * half : (y + 1) * half, :
-                    ]
-
-    def group_index(j):
-        return coarse_index(lax.div(j, per), lax.rem(j, per), True)
-
-    keep_sides(coarse)
-    loaded(2)
-
-    def own_index(i):
-        return group_index(brick_of(i, parity))
-
-    def inner_copy(i):
-        return remote(
-            inner_out.at[i], inner_in.at[i], pair_send_sem.at[0], pair_recv_sem.at[0], peer(1)
-        )
-
-    @pl.loop(0, own)
-    def _(i):
-        totals = local_product(coarse, own_index(i), w2)
-        opened[i, 0] = totals[0]
-        opened[i, 1] = totals[edge - 1]
-        value = jnp.maximum(jnp.concatenate(totals[1 : edge - 1], axis=0), 0.0).astype(BF16)
-        inner_out[i] = value
-        coarse2[brick_of(i, parity), 1 : edge - 1] = value.astype(F32).reshape(
-            (edge - 2,) + face
-        )
-        inner_copy(i).start()
-
-    def all_faces(side):
-        return remote(
-            side_in.at[side],
-            side_in.at[side],
-            side_send_sem.at[0, side],
-            side_recv_sem.at[0, side],
-            me + (LANES if side == 0 else -LANES),
-        )
-
-    @pl.when(has_down)
-    def _():
-        all_faces(0).wait_recv()
-        all_faces(1).wait_send()
-
-    @pl.when(has_up)
-    def _():
-        all_faces(1).wait_recv()
-        all_faces(0).wait_send()
-
-    pl.when(has_down)(lambda: far_to_smem(0).wait())
-    pl.when(has_up)(lambda: far_to_smem(1).wait())
-    pl.when(has_down)(lambda: place_far(0))
-    pl.when(has_up)(lambda: place_far(1))
-
-    def store_coarse(i, side, added):
-        value = jnp.maximum(opened[i, side] + added, 0.0).astype(BF16)
-        side_out2[i, side] = value
-        coarse2[brick_of(i, parity), side * (edge - 1)] = value.astype(F32).reshape(face)
-
-    outer_planes(own, high_x, low_x, own_index, w2, store_coarse)
-
-    def planes_to(side, k):
-        return remote(
-            side_out2,
-            side_in2.at[side, parity],
-            side_send_sem.at[1, side],
-            side_recv_sem.at[1, side],
-            peer(k) + (LANES if side == 0 else -LANES),
-        )
-
-    def all_planes(side):
-        return remote(
-            side_in2.at[side],
-            side_in2.at[side],
-            side_send_sem.at[1, side],
-            side_recv_sem.at[1, side],
-            me + (LANES if side == 0 else -LANES),
-        )
-
-    def send_planes(side):
-        for k in range(2):
-            planes_to(side, k).start()
-
-    pl.when(has_up)(lambda: send_planes(0))
-    pl.when(has_down)(lambda: send_planes(1))
-    outer_copy = remote(
-        side_out2, outer_in, pair_send_sem.at[1], pair_recv_sem.at[1], peer(1)
-    )
-    outer_copy.start()
-    loaded(3)
-
-    part = half * edge
-    strip = slots * part
-    tall = half + 2
-    column = tall * edge
-
-    def parent_of(s):
-        parent = fine_parent[s]
-        safe = jnp.maximum(parent, 0)
-        device, slot = owner_of(lax.div(safe, 8))
-        octant = lax.rem(safe, 8)
-        ox, oy = lax.div(octant, 4), lax.rem(lax.div(octant, 2), 2)
-        return coarse_index(lax.rem(device, LANES), slot, parent >= 0), ox, oy * half
-
-    remote(inner_out, inner_in, pair_send_sem.at[0], pair_recv_sem.at[0], peer(1)).wait()
-    outer_copy.wait()
+    remote(brick_out, brick_in, pair_send_sem, pair_recv_sem, peer(1)).wait()
     for i in range(own):
-        at = brick_of(i, 1 - parity)
-        coarse2[at, 1 : edge - 1] = inner_in[i].astype(F32).reshape((edge - 2,) + face)
-        coarse2[at, 0] = outer_in[i, 0].astype(F32).reshape(face)
-        coarse2[at, edge - 1] = outer_in[i, 1].astype(F32).reshape(face)
+        coarse2[brick_of(i, 1 - parity)] = brick_in[i].astype(F32).reshape(cube)
     keep_sides(coarse2)
     pad[0] = jnp.zeros(pad.shape[1:], F32)
     pad[edge + 1] = jnp.zeros(pad.shape[1:], F32)
@@ -944,9 +934,8 @@
             vmem((2, LANES, slots, half**2, width), BF16),
             vmem((bricks // 2, 2, plane, width), BF16),
             vmem((2, 2, bricks // 2, 2, plane, width), BF16),
-            vmem((bricks // 2, 2, plane, width), BF16),
-            vmem((bricks // 2, (edge - 2) * plane, width), BF16),
-            vmem((bricks // 2, (edge - 2) * plane, width), BF16),
+            vmem((bricks // 2, voxels, width), BF16),
+            vmem((bricks // 2, voxels, width), BF16),
             vmem((slots, half * half * 2 * edge, width), F32),
             dma((5,)),
             dma((5,)),
@@ -958,8 +947,8 @@
             dma(()),
             dma((3, 2)),
             dma((3, 2)),
-            dma((2,)),
-            dma((2,)),
+            dma(()),
+            dma(()),
             pltpu.SemaphoreType.REGULAR,
             dma(()),
             dma((2,)),

time: 25.2 us -> 23.9 us (0.948)
  Pallas kernels: 24.1 us -> 22.8 us
    pallas_call x1, Pallas kernels: 24.1 us -> 22.8 us  [per_device(): pl.pallas_call(functools.partial(kernel, n), out_shape=pltpu.VMEM((slots,...]
where the time goes in v5:
time: 23.9 us; the launch traced here: 23.6 us
  Pallas kernels  22.8 us (95%)
  local copies, waits for them, and re-layouts  0.8 us (3%)
    pallas_call x1, Pallas kernels, per_device(): pl.pallas_call(functools.partial(kernel, n), out_shape=pltpu.VMEM((slots,...  22.8 us
    unnamed x1, local copies, waits for them, and re-layouts  0.8 us

profile of v5, /device:TPU:5, one launch (start us, length us, event | category | flops | bytes accessed | tf_op | source)
XLA Modules:
  0.0 23.6 jit_solution(14126418506062368432)
XLA Ops:
  0.0 22.8 %shard_map.100 = bf16[4,512,128]{2,1,0:T(8,128)(2,1)S(1)} custom-call(s32[4,27]{1,0:T(4,128)} %fine_nbr_hbm.1, s32[2,4]{1,0:T(2,128)} %bitcast.13, s32[4]{0:T(128)} %fine_parent_hbm.1, s32[1,8]{1,0:T(1,128)} %child_hbm.1, s32[1,27]{1,0:T(1,128)} %nbr_hbm.1, bf16[4,512,128]{2,1,0:T(8,128)(2,1)} %bitcast.12, bf16[3,1152,128]{2,1,0:T(8,128)(2,1)} %bitcast.8, ...), custom_call_target="tpu_custom_call" | custom-call | tf_op jit(solution)/shard_map/pallas_call | solution.py:882
  22.8 0.8 %copy.12 = bf16[4,8,8,8,128]{4,3,2,1,0:T(8,128)(2,1)} copy(bf16[4,8,8,8,128]{4,3,2,1,0:T(8,128)(2,1)S(1)} %bitcast.7) | data formatting | bytes 1048576

commit v6 on v5

--- a/solution.py
+++ b/solution.py
@@ -10,6 +10,7 @@
 F32 = jnp.float32
 BF16 = jnp.bfloat16
 LANES = 4
+GROUP = 2
 MESH = pl.DeviceIdType.MESH
 
 
@@ -88,8 +89,7 @@
     far_children,
     coarse,
     coarse2,
-    low_x,
-    high_x,
+    ends,
     side_out,
     side_in,
     side_out2,
@@ -109,6 +109,8 @@
     side_recv_sem,
     pair_send_sem,
     pair_recv_sem,
+    hand_send_sem,
+    hand_recv_sem,
     ready_sem,
     meta_sem,
     far_sem,
@@ -224,6 +226,7 @@
     cube = (edge, edge, edge, width)
     face = (edge, edge, width)
     base = edge
+    high_x, low_x = ends.at[0], ends.at[1]
     padded = (edge + 2) * edge
     own_taps = range(9, 18)
     far_taps = (*range(9), *range(18, 27))
@@ -326,22 +329,30 @@
     def tread(value, row, rows):
         return value[row : row + rows, 0:width] + value[row + edge : row + edge + rows, width:]
 
-    def local_product(centre, index, weights):
-        assemble(pad, edge, centre, None, None, index, own_taps)
-        starts = [x * padded for x in range(edge)]
-        for x in range(edge):
-            shift(zs, x * padded, pad, x + 1, slice(None), edge + 2)
+    def local_product(centre, indices, weights):
+        rows = edge * padded
+        for i, index in enumerate(indices):
+            assemble(pad, edge, centre, None, None, index, own_taps)
+            for x in range(edge):
+                shift(zs, i * rows + x * padded, pad, x + 1, slice(None), edge + 2)
+        count = len(indices)
+        starts = [i * rows + x * padded for i in range(count) for x in range(edge)]
         two = dot(columns(zs, starts, plane), taps(weights, 0, 1))
-        third = stepped(zs, [padded], (edge - 1) * padded, weights[2])
-        totals = []
-        for x in range(edge):
-            total = two[x * plane : (x + 1) * plane, width : 2 * width]
-            if x > 0:
-                total = total + two[(x - 1) * plane : x * plane, 0:width]
-            if x < edge - 1:
-                total = total + tread(third, x * padded, plane)
-            totals.append(total)
-        return totals
+        inner = [i * rows + padded for i in range(count)]
+        third = stepped(zs, inner, (edge - 1) * padded, weights[2])
+        results = []
+        for i in range(count):
+            totals = []
+            for x in range(edge):
+                at = (i * edge + x) * plane
+                total = two[at : at + plane, width : 2 * width]
+                if x > 0:
+                    total = total + two[at - plane : at, 0:width]
+                if x < edge - 1:
+                    total = total + tread(third, (i * (edge - 1) + x) * padded, plane)
+                totals.append(total)
+            results.append(totals)
+        return results
 
     def outer_planes(count, lower, upper, index_of, weights, store):
         @pl.loop(0, count)
@@ -420,24 +431,29 @@
     start_pair(halo1[0], has_next, halo1[1], has_prev)
     loaded(1)
 
-    def encode(b):
-        totals = local_product(table, fine_index(b), w1)
-        opened[b, 0] = totals[0]
-        opened[b, 1] = totals[edge - 1]
-        value = rounded(jnp.concatenate(totals[1 : edge - 1], axis=0))
-        value = value.reshape((edge - 2,) + face)
-        enc[b, 1 : edge - 1] = value
-        pooled[member, b] = pool(value[1 : edge - 3], half - 2)
+    at_once = GROUP if slots % GROUP == 0 else 1
+
+    def encode(h):
+        bricks_of = [at_once * h + i for i in range(at_once)]
+        results = local_product(table, [fine_index(b) for b in bricks_of], w1)
+        for b, totals in zip(bricks_of, results):
+            opened[b, 0] = totals[0]
+            opened[b, 1] = totals[edge - 1]
+            value = rounded(jnp.concatenate(totals[1 : edge - 1], axis=0))
+            value = value.reshape((edge - 2,) + face)
+            enc[b, 1 : edge - 1] = value
+            pooled[member, b] = pool(value[1 : edge - 3], half - 2)
+        for b in bricks_of:
+            send_pooled(b)
 
     def send_pooled(b):
         for k in range(1, LANES):
             pool_copy(k, b).start()
 
 
-    @pl.loop(0, slots)
-    def _(b):
-        encode(b)
-        send_pooled(b)
+    @pl.loop(0, slots // at_once)
+    def _(h):
+        encode(h)
 
     finish_pair(halo1[0], has_next, halo1[1], has_prev)
     take_faces(face_in, below, above)
@@ -464,27 +480,44 @@
         octant = lax.rem(jnp.maximum(fine_parent[s], 0), 8)
         side_out[s] = own_out[s, lax.div(octant, 4)]
 
-    def face_to(side, lane):
+    parity = lax.rem(member, 2)
+
+    def face_to(side, h):
         return remote(
             side_out,
-            side_in.at[side, member],
+            side_in.at[side, parity, lax.div(member, 2)],
             side_send_sem.at[0, side],
             side_recv_sem.at[0, side],
-            first + (LANES if side == 0 else -LANES) + lane,
+            first + (LANES if side == 0 else -LANES) + 2 * h + parity,
         )
 
     def faces_to(side):
-        for lane in range(LANES):
-            face_to(side, lane).start()
+        for h in range(LANES // 2):
+            face_to(side, h).start()
+
+    def all_faces(side):
+        return remote(
+            side_in.at[side, 0],
+            side_in.at[side, 0],
+            side_send_sem.at[0, side],
+            side_recv_sem.at[0, side],
+            me + (LANES if side == 0 else -LANES),
+        )
+
+    def hand_over(side):
+        block_of = side_in.at[side, parity]
+        return remote(block_of, block_of, hand_send_sem.at[side], hand_recv_sem.at[side], peer(1))
 
     pl.semaphore_wait(ready_sem, LANES - 1)
+    pl.when(has_up)(lambda: faces_to(0))
+    pl.when(has_down)(lambda: faces_to(1))
     for s in range(slots):
         stage_faces(face_out2, enc, edge - 1, s)
 
     loaded(4)
 
     def decode_part(b):
-        totals = local_product(enc, fine_index(b), w4)
+        (totals,) = local_product(enc, [fine_index(b)], w4)
         acc[b] = jnp.concatenate(totals, axis=0)
 
     def run_decode(first, last):
@@ -492,11 +525,6 @@
         def _(b):
             decode_part(b)
 
-            @pl.when(b == 0)
-            def _():
-                pl.when(has_up)(lambda: faces_to(0))
-                pl.when(has_down)(lambda: faces_to(1))
-
     run_decode(0, slots)
 
     to_smem.wait()
@@ -509,6 +537,19 @@
     pl.when(has_up)(lambda: far_to_smem(1).start())
     for stage in range(2):
         all_pooled(stage).wait()
+
+    @pl.when(has_down)
+    def _():
+        all_faces(0).wait_recv()
+        all_faces(1).wait_send()
+        hand_over(0).start()
+
+    @pl.when(has_up)
+    def _():
+        all_faces(1).wait_recv()
+        all_faces(0).wait_send()
+        hand_over(1).start()
+
     start_pair(halo2[0], has_next, halo2[1], has_prev)
     for lane in range(LANES):
         for s in range(slots):
@@ -556,8 +597,6 @@
             high_x[bricks + j] = source[j, edge - 1]
 
     own = bricks // 2
-    parity = lax.rem(member, 2)
-
     def brick_of(i, odd):
         lane, slot = halves(i, per)
         return (2 * lane + odd) * per + slot
@@ -566,7 +605,7 @@
         start = 2 * bricks * side
         for lane in range(LANES):
             for s in range(slots):
-                far_children[side, lane * slots + s] = side_in[side, lane, s].astype(F32)
+                far_children[side, lane * slots + s] = side_in[side, lane % 2, lane // 2, s].astype(F32)
         far_children[side, LANES * slots] = jnp.zeros((cells, width), F32)
 
         @pl.loop(0, bricks)
@@ -585,29 +624,14 @@
         return coarse_index(*halves(j, per), True)
 
     keep_sides(coarse)
-    def all_faces(side):
-        return remote(
-            side_in.at[side],
-            side_in.at[side],
-            side_send_sem.at[0, side],
-            side_recv_sem.at[0, side],
-            me + (LANES if side == 0 else -LANES),
-        )
-
-    @pl.when(has_down)
-    def _():
-        all_faces(0).wait_recv()
-        all_faces(1).wait_send()
-
-    @pl.when(has_up)
-    def _():
-        all_faces(1).wait_recv()
-        all_faces(0).wait_send()
-
-    pl.when(has_down)(lambda: far_to_smem(0).wait())
-    pl.when(has_up)(lambda: far_to_smem(1).wait())
-    pl.when(has_down)(lambda: place_far(0))
-    pl.when(has_up)(lambda: place_far(1))
+    def far_planes():
+        pl.when(has_down)(lambda: hand_over(0).wait())
+        pl.when(has_up)(lambda: hand_over(1).wait())
+        pl.when(has_down)(lambda: far_to_smem(0).wait())
+        pl.when(has_up)(lambda: far_to_smem(1).wait())
+        pl.when(has_down)(lambda: place_far(0))
+        pl.when(has_up)(lambda: place_far(1))
+
 
     loaded(2)
 
@@ -638,19 +662,25 @@
     @pl.loop(0, own)
     def _(i):
         index = own_index(i)
-        totals = local_product(coarse, index, w2)
+        (totals,) = local_product(coarse, [index], w2)
+        opened[i, 0] = totals[0]
+        opened[i, 1] = totals[edge - 1]
+        value = jnp.maximum(jnp.concatenate(totals[1 : edge - 1], axis=0), 0.0).astype(BF16)
+        brick_out[i, plane : (edge - 1) * plane] = value
+        coarse2[brick_of(i, parity), 1 : edge - 1] = value.astype(F32).reshape(
+            (edge - 2,) + face
+        )
+        pl.when(i == 0)(far_planes)
         assemble(pad, edge, None, high_x, low_x, index, far_taps)
         for side in range(2):
             shift(zfar, side * padded, pad, side * (edge + 1), slice(None), edge + 2)
         for side in range(2):
             added = stepped(zfar, [side * padded], padded, w2[2 * side])
             at = side * (edge - 1)
-            totals[at] = totals[at] + tread(added, 0, plane)
-        value = jnp.maximum(jnp.concatenate(totals, axis=0), 0.0).astype(BF16)
-        side_out2[i, 0] = value[0:plane]
-        side_out2[i, 1] = value[(edge - 1) * plane :]
-        brick_out[i] = value
-        coarse2[brick_of(i, parity)] = value.astype(F32).reshape(cube)
+            value = jnp.maximum(opened[i, side] + tread(added, 0, plane), 0.0).astype(BF16)
+            side_out2[i, side] = value
+            brick_out[i, at * plane : (at + 1) * plane] = value
+            coarse2[brick_of(i, parity), at] = value.astype(F32).reshape(face)
 
         def send_planes(side):
             for k in range(2):
@@ -673,7 +703,7 @@
         lane, slot = halves(jnp.clip(safe // 8 - group * bricks, 0, bricks - 1), per)
         octant = safe % 8
         ox, oy = lax.div(octant, 4), lax.rem(lax.div(octant, 2), 2)
-        return coarse_index(lane, slot, parent >= 0), ox, oy * half
+        return lane, slot, ox, oy * half
 
     strips = 4
     span = width // strips
@@ -703,7 +733,8 @@
 
     @pl.loop(0, slots)
     def _(s):
-        index, ox, oy = parent_of(s)
+        lane, slot, ox, oy = parent_of(s)
+        index = coarse_index(lane, slot, fine_parent[s] >= 0)
         assemble(pad, edge, coarse2, None, None, index, own_taps)
         for x in range(tall):
             row = pl.multiple_of((s * tall + x) * column, edge)
@@ -725,14 +756,18 @@
                 + tread(third, (s * half + x) * column, part)
             )
 
-    finish_pair(halo2[0], has_next, halo2[1], has_prev)
-    take_faces(face_in2, below, above)
-
-    def store_part(b, side, added):
-        at = side * (edge - 1) * plane
-        acc[b, at : at + plane] = acc[b, at : at + plane] + added
-
-    outer_planes(slots, below, above, fine_index, w4, store_part)
+    def lift(s, x, value):
+        piece = rounded(value)
+        oz = lax.rem(jnp.maximum(fine_parent[s], 0), 2)
+        start = x * 2 * part
+        spread[s, pl.ds(start, part, stride=2), :] = piece
+        spread[s, pl.ds(start + 1, part, stride=2), :] = piece
+        for y in range(half):
+            utab[s, x, y] = spread[s, pl.ds(start + (2 * y + oz) * edge, edge), :]
+
+    for s in range(slots):
+        for x in range(1, half - 1):
+            lift(s, x, dacc[x * strip + s * part : x * strip + (s + 1) * part, :])
     @pl.when(has_down)
     def _():
         all_planes(0).wait_recv()
@@ -753,10 +788,17 @@
 
     @pl.loop(0, slots)
     def _(s):
-        index, ox, oy = parent_of(s)
-        assemble(pad, edge, None, high_x, low_x, index, far_taps)
+        lane, slot, ox, oy = parent_of(s)
+        live = fine_parent[s] >= 0
+        for k in range(9):
+            value = meta_s[lane, per + slot, ox * 18 + k]
+            at = jnp.clip(value - (group - 1) * bricks, 0, 3 * bricks - 1)
+            at = jnp.where((value >= 0) & live, at, 3 * bricks)
+            dy, dz = k // 3 - 1, k % 3 - 1
+            piece = ends[ox, at, pick(dy, edge), pick(dz, edge), :]
+            pad[0, place(dy, edge, 1), place(dz, edge, base), :] = piece
         row = pl.multiple_of(s * column, edge)
-        shift(zfar, row, pad, ox * (edge + 1), pl.ds(oy, tall), tall)
+        shift(zfar, row, pad, 0, pl.ds(oy, tall), tall)
 
     far = dot(
         columns(zfar, [s * column for s in range(slots)], part),
@@ -766,21 +808,11 @@
     picks[1] = jnp.zeros((strip, width), F32)
     picks[2] = far[:, width : 2 * width]
     for s in range(slots):
-        _, ox, _ = parent_of(s)
+        ox = parent_of(s)[2]
         rows = slice(s * part, (s + 1) * part)
-        low = picks[ox, rows]
-        high = picks[ox + 1, rows]
-        pieces = [dacc[x * strip + s * part : x * strip + (s + 1) * part, :] for x in range(half)]
-        pieces[0] = pieces[0] + low
-        pieces[half - 1] = pieces[half - 1] + high
-        piece = rounded(jnp.concatenate(pieces, axis=0))
-        oz = lax.rem(jnp.maximum(fine_parent[s], 0), 2)
-        spread[s, pl.ds(0, half * part, stride=2), :] = piece
-        spread[s, pl.ds(1, half * part, stride=2), :] = piece
-        for x in range(half):
-            for y in range(half):
-                start = ((x * half + y) * 2 + oz) * edge
-                utab[s, x, y] = spread[s, pl.ds(start, edge), :]
+        lift(s, 0, dacc[rows, :] + picks[ox, rows])
+        last = (half - 1) * strip + s * part
+        lift(s, half - 1, dacc[last : last + part, :] + picks[ox + 1, rows])
         stage_faces(face_out3, utab, half - 1, s)
     start_pair(halo3[0], has_next, halo3[1], has_prev)
 
@@ -826,6 +858,14 @@
             else:
                 acc[b, rows] = total
 
+    finish_pair(halo2[0], has_next, halo2[1], has_prev)
+    take_faces(face_in2, below, above)
+
+    def store_part(b, side, added):
+        at = side * (edge - 1) * plane
+        acc[b, at : at + plane] = acc[b, at : at + plane] + added
+
+    outer_planes(slots, below, above, fine_index, w4, store_part)
     finish_pair(halo3[0], has_next, halo3[1], has_prev)
     take_faces(face_in3, ubelow, uabove)
 
@@ -895,7 +935,7 @@
             vmem((2, 6 * width, 4 * width), BF16),
             vmem((edge + 2, edge + 2, 3 * edge, width), F32),
             vmem((half + 2, half + 2, 3 * edge, width), F32),
-            vmem((3, edge * padded + edge, width), BF16),
+            vmem((3, GROUP * edge * padded + edge, width), BF16),
             vmem((3, 2 * max(slots, bricks) * padded + edge, width), BF16),
             vmem((3, slots * tall * tall * edge + edge, width), BF16),
             vmem((3, slots * tall * tall * edge, width), BF16),
@@ -928,10 +968,9 @@
             vmem((2, LANES * slots + 1, half**2, width), F32),
             vmem((bricks + 1,) + cube, F32),
             vmem((bricks + 1,) + cube, F32),
-            vmem((3 * bricks + 1,) + face, F32),
-            vmem((3 * bricks + 1,) + face, F32),
+            vmem((2, 3 * bricks + 1) + face, F32),
             vmem((slots, half**2, width), BF16),
-            vmem((2, LANES, slots, half**2, width), BF16),
+            vmem((2, 2, LANES // 2, slots, half**2, width), BF16),
             vmem((bricks // 2, 2, plane, width), BF16),
             vmem((2, 2, bricks // 2, 2, plane, width), BF16),
             vmem((bricks // 2, voxels, width), BF16),
@@ -949,6 +988,8 @@
             dma((3, 2)),
             dma(()),
             dma(()),
+            dma((2,)),
+            dma((2,)),
             pltpu.SemaphoreType.REGULAR,
             dma(()),
             dma((2,)),

time: 23.9 us -> 23.5 us (0.983)
  Pallas kernels: 22.8 us -> 22.5 us
    pallas_call x1, Pallas kernels: 22.8 us -> 22.5 us  [per_device(): pl.pallas_call(functools.partial(kernel, n), out_shape=pltpu.VMEM((slots,...]
where the time goes in v6:
time: 23.5 us; the launch traced here: 23.3 us
  Pallas kernels  22.5 us (96%)
  local copies, waits for them, and re-layouts  0.8 us (3%)
    pallas_call x1, Pallas kernels, per_device(): pl.pallas_call(functools.partial(kernel, n), out_shape=pltpu.VMEM((slots,...  22.5 us
    unnamed x1, local copies, waits for them, and re-layouts  0.8 us

profile of v6, /device:TPU:5, one launch (start us, length us, event | category | flops | bytes accessed | tf_op | source)
XLA Modules:
  0.0 23.3 jit_solution(17573435283513161445)
XLA Ops:
  0.0 22.5 %shard_map.100 = bf16[4,512,128]{2,1,0:T(8,128)(2,1)S(1)} custom-call(s32[4,27]{1,0:T(4,128)} %fine_nbr_hbm.1, s32[2,4]{1,0:T(2,128)} %bitcast.13, s32[4]{0:T(128)} %fine_parent_hbm.1, s32[1,8]{1,0:T(1,128)} %child_hbm.1, s32[1,27]{1,0:T(1,128)} %nbr_hbm.1, bf16[4,512,128]{2,1,0:T(8,128)(2,1)} %bitcast.12, bf16[3,1152,128]{2,1,0:T(8,128)(2,1)} %bitcast.8, ...), custom_call_target="tpu_custom_call" | custom-call | tf_op jit(solution)/shard_map/pallas_call | solution.py:922
  22.5 0.8 %copy.12 = bf16[4,8,8,8,128]{4,3,2,1,0:T(8,128)(2,1)} copy(bf16[4,8,8,8,128]{4,3,2,1,0:T(8,128)(2,1)S(1)} %bitcast.7) | data formatting | bytes 1048576

commit v7 on v6

--- a/solution.py
+++ b/solution.py
@@ -112,8 +112,6 @@
     hand_send_sem,
     hand_recv_sem,
     ready_sem,
-    meta_sem,
-    far_sem,
 ):
     slots, edge = out_ref.shape[0], enc.shape[1]
     plane = edge * edge
@@ -194,14 +192,14 @@
         up = remote(
             outgoing.at[0],
             incoming.at[0],
-            face_send_sem.at[phase, 0],
+            face_send_sem.at[0],
             face_recv_sem.at[phase, 0],
             me + 1,
         )
         down = remote(
             outgoing.at[1],
             incoming.at[1],
-            face_send_sem.at[phase, 1],
+            face_send_sem.at[1],
             face_recv_sem.at[phase, 1],
             me - 1,
         )
@@ -387,16 +385,20 @@
 
     def pool_copy(k, b):
         source = pooled_out.at[member] if b is None else pooled.at[member, b]
-        stage = int(b is None)
+        stage = 1 if b is None else 2 * (k - 1)
         return remote(
             source, source, pool_send_sem.at[stage], pool_recv_sem.at[stage], peer(k)
         )
 
     def all_pooled(stage):
-        source = (pooled, pooled_out)[stage].at[0 : LANES - 1]
+        source = (pooled.at[0:2], pooled_out.at[0 : LANES - 1], pooled.at[0])[stage]
         return remote(
             source, source, pool_send_sem.at[stage], pool_recv_sem.at[stage], peer(1)
         )
+
+    def pass_pooled():
+        source = pooled.at[member ^ 2]
+        return remote(source, source, pool_send_sem.at[0], pool_recv_sem.at[0], peer(1))
 
     def pool(value, count):
         pairs = value.reshape(count, 2, half, 2, edge, width)
@@ -410,14 +412,14 @@
         up = remote(
             outgoing,
             incoming.at[0],
-            side_send_sem.at[phase, 0],
+            side_send_sem.at[min(phase, 1), 0],
             side_recv_sem.at[phase, 0],
             me + LANES,
         )
         down = remote(
             outgoing,
             incoming.at[1],
-            side_send_sem.at[phase, 1],
+            side_send_sem.at[min(phase, 1), 1],
             side_recv_sem.at[phase, 1],
             me - LANES,
         )
@@ -447,7 +449,7 @@
             send_pooled(b)
 
     def send_pooled(b):
-        for k in range(1, LANES):
+        for k in (2, 1):
             pool_copy(k, b).start()
 
 
@@ -460,7 +462,7 @@
 
     every_meta = meta.at[0 : LANES - 1]
     remote(every_meta, every_meta, meta_send_sem, meta_recv_sem, peer(1)).wait()
-    to_smem = pltpu.make_async_copy(meta, meta_s, meta_sem)
+    to_smem = pltpu.make_async_copy(meta, meta_s, small_sem.at[0])
     to_smem.start()
     hop_meta = side_copies(meta, meta_far, 2)
     start_pair(hop_meta[0], has_up, hop_meta[1], has_down)
@@ -525,18 +527,24 @@
         def _(b):
             decode_part(b)
 
+            @pl.when(b == max(slots - 2, 0))
+            def _():
+                all_pooled(2).wait_recv()
+                pass_pooled().start()
+
     run_decode(0, slots)
 
     to_smem.wait()
     finish_pair(hop_meta[0], has_up, hop_meta[1], has_down)
 
     def far_to_smem(side):
-        return pltpu.make_async_copy(meta_far.at[side], meta_far_s.at[side], far_sem.at[side])
+        return pltpu.make_async_copy(meta_far.at[side], meta_far_s.at[side], small_sem.at[1 + side])
 
     pl.when(has_down)(lambda: far_to_smem(0).start())
     pl.when(has_up)(lambda: far_to_smem(1).start())
     for stage in range(2):
         all_pooled(stage).wait()
+    all_pooled(2).wait_send()
 
     @pl.when(has_down)
     def _():
@@ -645,7 +653,7 @@
         return remote(
             side_out2.at[i],
             side_in2.at[side, parity, i],
-            side_send_sem.at[1, side],
+            side_send_sem.at[0, side],
             side_recv_sem.at[1, side],
             peer(k) + (LANES if side == 0 else -LANES),
         )
@@ -654,7 +662,7 @@
         return remote(
             side_in2.at[side],
             side_in2.at[side],
-            side_send_sem.at[1, side],
+            side_send_sem.at[0, side],
             side_recv_sem.at[1, side],
             me + (LANES if side == 0 else -LANES),
         )
@@ -978,21 +986,19 @@
             vmem((slots, half * half * 2 * edge, width), F32),
             dma((5,)),
             dma((5,)),
+            dma((2,)),
             dma((3, 2)),
-            dma((3, 2)),
-            dma((2,)),
-            dma((2,)),
+            dma((3,)),
+            dma((3,)),
             dma(()),
             dma(()),
-            dma((3, 2)),
+            dma((2, 2)),
             dma((3, 2)),
             dma(()),
             dma(()),
             dma((2,)),
             dma((2,)),
             pltpu.SemaphoreType.REGULAR,
-            dma(()),
-            dma((2,)),
         ],
         compiler_params=pltpu.CompilerParams(
             collective_id=0, has_side_effects=True, vmem_limit_bytes=60 * 1024 * 1024

time: 23.5 us -> 23.4 us (level)
  no operation moved by 1% of the time
where the time goes in v7:
time: 23.4 us; the launch traced here: 23.2 us
  Pallas kernels  22.4 us (96%)
  local copies, waits for them, and re-layouts  0.8 us (3%)
    pallas_call x1, Pallas kernels, per_device(): pl.pallas_call(functools.partial(kernel, n), out_shape=pltpu.VMEM((slots,...  22.4 us
    unnamed x1, local copies, waits for them, and re-layouts  0.8 us

profile of v7, /device:TPU:5, one launch (start us, length us, event | category | flops | bytes accessed | tf_op | source)
XLA Modules:
  0.0 23.2 jit_solution(956150309085949684)
XLA Ops:
  0.0 22.4 %shard_map.100 = bf16[4,512,128]{2,1,0:T(8,128)(2,1)S(1)} custom-call(s32[4,27]{1,0:T(4,128)} %fine_nbr_hbm.1, s32[2,4]{1,0:T(2,128)} %bitcast.13, s32[4]{0:T(128)} %fine_parent_hbm.1, s32[1,8]{1,0:T(1,128)} %child_hbm.1, s32[1,27]{1,0:T(1,128)} %nbr_hbm.1, bf16[4,512,128]{2,1,0:T(8,128)(2,1)} %bitcast.12, bf16[3,1152,128]{2,1,0:T(8,128)(2,1)} %bitcast.8, ...), custom_call_target="tpu_custom_call" | custom-call | tf_op jit(solution)/shard_map/pallas_call | solution.py:930
  22.4 0.8 %copy.12 = bf16[4,8,8,8,128]{4,3,2,1,0:T(8,128)(2,1)} copy(bf16[4,8,8,8,128]{4,3,2,1,0:T(8,128)(2,1)S(1)} %bitcast.7) | data formatting | bytes 1048576

commit v8 on v7

--- a/solution.py
+++ b/solution.py
@@ -445,8 +445,6 @@
             value = value.reshape((edge - 2,) + face)
             enc[b, 1 : edge - 1] = value
             pooled[member, b] = pool(value[1 : edge - 3], half - 2)
-        for b in bricks_of:
-            send_pooled(b)
 
     def send_pooled(b):
         for k in (2, 1):
@@ -456,6 +454,9 @@
     @pl.loop(0, slots // at_once)
     def _(h):
         encode(h)
+
+    for b in range(slots):
+        send_pooled(b)
 
     finish_pair(halo1[0], has_next, halo1[1], has_prev)
     take_faces(face_in, below, above)

time: 23.4 us -> 23.3 us (level)
  no operation moved by 1% of the time
where the time goes in v8:
time: 23.3 us; the launch traced here: 23.2 us
  Pallas kernels  22.4 us (96%)
  local copies, waits for them, and re-layouts  0.8 us (3%)
    pallas_call x1, Pallas kernels, per_device(): pl.pallas_call(functools.partial(kernel, n), out_shape=pltpu.VMEM((slots,...  22.4 us
    unnamed x1, local copies, waits for them, and re-layouts  0.8 us

profile of v8, /device:TPU:5, one launch (start us, length us, event | category | flops | bytes accessed | tf_op | source)
XLA Modules:
  0.0 23.2 jit_solution(5582103935206124921)
XLA Ops:
  0.0 22.4 %shard_map.100 = bf16[4,512,128]{2,1,0:T(8,128)(2,1)S(1)} custom-call(s32[4,27]{1,0:T(4,128)} %fine_nbr_hbm.1, s32[2,4]{1,0:T(2,128)} %bitcast.13, s32[4]{0:T(128)} %fine_parent_hbm.1, s32[1,8]{1,0:T(1,128)} %child_hbm.1, s32[1,27]{1,0:T(1,128)} %nbr_hbm.1, bf16[4,512,128]{2,1,0:T(8,128)(2,1)} %bitcast.12, bf16[3,1152,128]{2,1,0:T(8,128)(2,1)} %bitcast.8, ...), custom_call_target="tpu_custom_call" | custom-call | tf_op jit(solution)/shard_map/pallas_call | solution.py:931
  22.4 0.8 %copy.12 = bf16[4,8,8,8,128]{4,3,2,1,0:T(8,128)(2,1)} copy(bf16[4,8,8,8,128]{4,3,2,1,0:T(8,128)(2,1)S(1)} %bitcast.7) | data formatting | bytes 1048576

commit v9 on v8

--- a/solution.py
+++ b/solution.py
@@ -559,7 +559,6 @@
         all_faces(0).wait_send()
         hand_over(1).start()
 
-    start_pair(halo2[0], has_next, halo2[1], has_prev)
     for lane in range(LANES):
         for s in range(slots):
             at = lane * slots + s
@@ -737,6 +736,7 @@
     for i in range(own):
         coarse2[brick_of(i, 1 - parity)] = brick_in[i].astype(F32).reshape(cube)
     keep_sides(coarse2)
+    start_pair(halo2[0], has_next, halo2[1], has_prev)
     pad[0] = jnp.zeros(pad.shape[1:], F32)
     pad[edge + 1] = jnp.zeros(pad.shape[1:], F32)
 

time: 23.3 us -> 23.3 us (level)
  no operation moved by 1% of the time
where the time goes in v9:
time: 23.3 us; the launch traced here: 23.2 us
  Pallas kernels  22.4 us (96%)
  local copies, waits for them, and re-layouts  0.8 us (3%)
    pallas_call x1, Pallas kernels, per_device(): pl.pallas_call(functools.partial(kernel, n), out_shape=pltpu.VMEM((slots,...  22.4 us
    unnamed x1, local copies, waits for them, and re-layouts  0.8 us

profile of v9, /device:TPU:5, one launch (start us, length us, event | category | flops | bytes accessed | tf_op | source)
XLA Modules:
  0.0 23.2 jit_solution(4814098471677800274)
XLA Ops:
  0.0 22.4 %shard_map.100 = bf16[4,512,128]{2,1,0:T(8,128)(2,1)S(1)} custom-call(s32[4,27]{1,0:T(4,128)} %fine_nbr_hbm.1, s32[2,4]{1,0:T(2,128)} %bitcast.13, s32[4]{0:T(128)} %fine_parent_hbm.1, s32[1,8]{1,0:T(1,128)} %child_hbm.1, s32[1,27]{1,0:T(1,128)} %nbr_hbm.1, bf16[4,512,128]{2,1,0:T(8,128)(2,1)} %bitcast.12, bf16[3,1152,128]{2,1,0:T(8,128)(2,1)} %bitcast.8, ...), custom_call_target="tpu_custom_call" | custom-call | tf_op jit(solution)/shard_map/pallas_call | solution.py:931
  22.4 0.8 %copy.12 = bf16[4,8,8,8,128]{4,3,2,1,0:T(8,128)(2,1)} copy(bf16[4,8,8,8,128]{4,3,2,1,0:T(8,128)(2,1)S(1)} %bitcast.7) | data formatting | bytes 1048576
